TPU v7x, 32 devices: a whole 2x2x4 slice. The times are simulated.
32 devices in a mesh: dp: 8 (over z, x), tensor: 4 (over y, core).
Axes of the slice: x: 2, y: 2, z: 4, core: 2. Of those that a mesh axis runs over, the one named last changes fastest.
Arguments:
- inputs: bfloat16 [16384, 768], P(('dp', 'tensor')), may hold values from -6 to 6
- teacher: bfloat16 [16384, 768], P(('dp', 'tensor')), may hold values from -6 to 6
- lengths: int32 [8], P('dp'), may hold values from 512 to 2048
- buckets: int32 [4096], replicated, may hold values from 0 to 31
- gain_attn: bfloat16 [768], replicated, may hold values from 0.25 to 1.75
- w_query: bfloat16 [768, 768], P(None, 'tensor'), may hold values from -0.4375 to 0.4375
- w_key: bfloat16 [768, 768], P(None, 'tensor'), may hold values from -0.21875 to 0.21875
- w_value: bfloat16 [768, 768], P(None, 'tensor'), may hold values from -0.21875 to 0.21875
- w_out: bfloat16 [768, 768], P('tensor'), may hold values from -1.75 to 1.75
- bias_table: bfloat16 [32, 12], P(None, 'tensor'), may hold values from -4 to 4
- gain_ff: bfloat16 [768], replicated, may hold values from 0.25 to 1.75
- w_gate: bfloat16 [768, 2048], P(None, 'tensor'), may hold values from -0.21875 to 0.21875
- w_up: bfloat16 [768, 2048], P(None, 'tensor'), may hold values from -0.21875 to 0.21875
- w_down: bfloat16 [2048, 768], P('tensor'), may hold values from -0.125 to 0.125
Outputs:
- activations: bfloat16 [16384, 768], P(('dp', 'tensor'))
- loss: float32 [], replicated
- grad_inputs: float32 [16384, 768], P(('dp', 'tensor'))
- grad_gain_attn: float32 [768], replicated
- grad_query: float32 [768, 768], P(None, 'tensor')
- grad_key: float32 [768, 768], P(None, 'tensor')
- grad_value: float32 [768, 768], P(None, 'tensor')
- grad_out: float32 [768, 768], P('tensor')
- grad_table: float32 [32, 12], P(None, 'tensor')
- grad_gain_ff: float32 [768], replicated
- grad_gate: float32 [768, 2048], P(None, 'tensor')
- grad_up: float32 [768, 2048], P(None, 'tensor')
- grad_down: float32 [2048, 768], P('tensor')
All inputs are finite; a program needn't handle non-finite values.
Results may differ from a plain program's by a relative error of at most 0.015.
The roundings to bfloat16 on the way count: a program that leaves them out, or rounds other values in their place, can miss the bound.
Values may be sent and summed in bfloat16 or wider, within the bound.
A program may use at most 320 MiB of HBM per device.

v0:
```python
import jax
import jax.numpy as jnp
from jax import lax
from jax.sharding import PartitionSpec as P

QBLOCK = 512


eps_norm = 1e-06
masked_score = -1e30
highest = lax.Precision.HIGHEST
contract_rows = (((0,), (0,)), ((), ()))
contract_cols = (((1,), (1,)), ((), ()))
contract_table = (((0,), (1,)), ((), ()))


def row_norm(values, gain):
    inverse = lax.rsqrt(jnp.mean(values * values, axis=-1, keepdims=True) + eps_norm)
    return values * inverse * gain


def geglu_mask(gate_values, up_values, keep_column):
    return keep_column * jax.nn.gelu(gate_values, approximate=True) * up_values


def valid_mask(lengths, first_row, row_count, seq_len):
    positions = first_row + lax.iota(jnp.int32, row_count)
    owners = positions // seq_len
    within = positions % seq_len
    chosen = owners[:, None] == lax.iota(jnp.int32, lengths.shape[0])[None, :]
    limits = jnp.sum(jnp.where(chosen, lengths[None, :], 0), axis=1)
    return (within < limits).astype(jnp.float32)


def bucket_rows(buckets, bias_table):
    one_hot = (buckets[:, None] == lax.iota(jnp.int32, bias_table.shape[0])[None, :]).astype(
        jnp.float32
    )
    relative = lax.dot_general(
        bias_table.astype(jnp.float32), one_hot, contract_table, precision=highest
    )
    return (one_hot, relative)


def band_matrix(window, block_rows, seq_len):
    heads_here = window.shape[0]
    span = seq_len + block_rows - 1
    tiled = jnp.tile(window, (1, block_rows + 1))
    tiled = tiled[:, block_rows - 1 : block_rows - 1 + block_rows * (span - 1)]
    return tiled.reshape(heads_here, block_rows, span - 1)[:, :, :seq_len]


def make_bands(relative, block_rows, seq_len):
    pieces = []
    for block_index in range(seq_len // block_rows):
        first_row = block_index * block_rows
        start = seq_len - first_row - block_rows + 1
        window = relative[:, start : start + seq_len + block_rows - 1]
        pieces.append(band_matrix(window, block_rows, seq_len))
    return jnp.stack(pieces, axis=1)


def attend_head(query_head, key_head, value_head, keep_seq, length, bands_head, block_rows, scale):
    seq_len, head_dim = query_head.shape
    key_live = lax.iota(jnp.int32, seq_len) < length

    def one_block(step_index, totals):
        mixed_rows, log_sums = totals
        first_row = step_index * block_rows
        query_block = lax.dynamic_slice_in_dim(query_head, first_row, block_rows, 0)
        band = lax.dynamic_index_in_dim(bands_head, step_index, 0, keepdims=False)
        raw_scores = lax.dot_general(
            query_block, key_head, contract_cols, preferred_element_type=jnp.float32
        )
        scores = jnp.where(key_live[None, :], raw_scores * scale + band, masked_score)
        row_max = jnp.max(scores, axis=-1, keepdims=True)
        expos = jnp.exp(scores - row_max)
        row_total = jnp.sum(expos, axis=-1, keepdims=True)
        probs = (expos / row_total).astype(jnp.bfloat16)
        mixed = jnp.dot(probs, value_head, preferred_element_type=jnp.float32)
        keep_block = lax.dynamic_slice_in_dim(keep_seq, first_row, block_rows, 0)
        mixed = (mixed * keep_block[:, None]).astype(jnp.bfloat16)
        mixed_rows = lax.dynamic_update_slice_in_dim(mixed_rows, mixed, first_row, 0)
        log_sums = lax.dynamic_update_slice_in_dim(
            log_sums, (row_max + jnp.log(row_total))[:, 0], first_row, 0
        )
        return (mixed_rows, log_sums)

    initial = (jnp.zeros((seq_len, head_dim), jnp.bfloat16), jnp.zeros((seq_len,), jnp.float32))
    return lax.fori_loop(0, seq_len // block_rows, one_block, initial)


def attend_head_back(
    query_head,
    key_head,
    value_head,
    grad_head,
    log_sums,
    length,
    bands_head,
    grad_bands_head,
    block_rows,
    scale,
):
    seq_len, head_dim = query_head.shape
    key_live = lax.iota(jnp.int32, seq_len) < length

    def one_block(step_index, totals):
        grad_query, grad_key, grad_value, grad_band = totals
        first_row = step_index * block_rows
        query_block = lax.dynamic_slice_in_dim(query_head, first_row, block_rows, 0)
        grad_block = lax.dynamic_slice_in_dim(grad_head, first_row, block_rows, 0)
        band = lax.dynamic_index_in_dim(bands_head, step_index, 0, keepdims=False)
        raw_scores = lax.dot_general(
            query_block, key_head, contract_cols, preferred_element_type=jnp.float32
        )
        scores = jnp.where(key_live[None, :], raw_scores * scale + band, masked_score)
        block_sums = lax.dynamic_slice_in_dim(log_sums, first_row, block_rows, 0)
        probs = jnp.exp(scores - block_sums[:, None])
        grad_value = grad_value + lax.dot_general(
            probs.astype(jnp.bfloat16),
            grad_block,
            contract_rows,
            preferred_element_type=jnp.float32,
        )
        grad_probs = lax.dot_general(
            grad_block, value_head, contract_cols, preferred_element_type=jnp.float32
        )
        inner = jnp.sum(probs * grad_probs, axis=-1, keepdims=True)
        grad_scores = (probs * (grad_probs - inner)).astype(jnp.bfloat16)
        grad_query_block = (
            jnp.dot(grad_scores, key_head, preferred_element_type=jnp.float32) * scale
        )
        grad_query = lax.dynamic_update_slice_in_dim(
            grad_query, grad_query_block.astype(jnp.bfloat16), first_row, 0
        )
        grad_key = (
            grad_key
            + lax.dot_general(
                grad_scores, query_block, contract_rows, preferred_element_type=jnp.float32
            )
            * scale
        )
        current = lax.dynamic_index_in_dim(grad_band, step_index, 0, keepdims=True)
        grad_band = lax.dynamic_update_slice_in_dim(
            grad_band, current + grad_scores.astype(jnp.float32)[None], step_index, 0
        )
        return (grad_query, grad_key, grad_value, grad_band)

    initial = (
        jnp.zeros((seq_len, head_dim), jnp.bfloat16),
        jnp.zeros((seq_len, head_dim), jnp.float32),
        jnp.zeros((seq_len, head_dim), jnp.float32),
        grad_bands_head,
    )
    return lax.fori_loop(0, seq_len // block_rows, one_block, initial)


def on_device(
    inputs,
    teacher,
    lengths,
    buckets,
    gain_attn,
    w_query,
    w_key,
    w_value,
    w_out,
    bias_table,
    gain_ff,
    w_gate,
    w_up,
    w_down,
):
    row_count, model_width = inputs.shape
    group_size = lax.axis_size("tensor")
    seq_len = buckets.shape[0] // 2
    all_rows = row_count * group_size
    block_rows = QBLOCK
    local_width = w_query.shape[1]
    heads_here = bias_table.shape[1]
    head_dim = local_width // heads_here
    ff_width = w_gate.shape[1]
    scale = head_dim ** (-0.5)
    my_first = lax.axis_index("tensor") * row_count
    keep_mine = valid_mask(lengths, my_first, row_count, seq_len)
    keep_all = valid_mask(lengths, 0, all_rows, seq_len)
    one_hot, relative = bucket_rows(buckets, bias_table)
    bands = make_bands(relative, block_rows, seq_len)
    gain_a = gain_attn.astype(jnp.float32)
    gain_f = gain_ff.astype(jnp.float32)
    source = inputs.astype(jnp.float32)
    normed = row_norm(source, gain_a).astype(jnp.bfloat16)
    normed_all = lax.all_gather(normed, "tensor", axis=0, tiled=True)
    w_joint = jnp.concatenate([w_query, w_key, w_value], axis=1)

    def head_proj(weight, head):
        columns = weight[:, head * head_dim : (head + 1) * head_dim]
        return jnp.dot(normed_all, columns, preferred_element_type=jnp.float32).astype(jnp.bfloat16)

    query_heads = [head_proj(w_query, head) for head in range(heads_here)]
    key_heads = [head_proj(w_key, head) for head in range(heads_here)]
    value_heads = [head_proj(w_value, head) for head in range(heads_here)]
    seq_index = 0
    head_mixed = []
    head_sums = []
    for head in range(heads_here):
        mixed_head, sums_head = attend_head(
            query_heads[head],
            key_heads[head],
            value_heads[head],
            keep_all,
            lengths[seq_index],
            bands[head],
            block_rows,
            scale,
        )
        head_mixed.append(mixed_head)
        head_sums.append(sums_head)
    mixed_parts = jnp.concatenate(head_mixed, axis=1)
    sums_parts = [head_sums]
    middle = source + lax.psum_scatter(
        jnp.dot(mixed_parts, w_out, preferred_element_type=jnp.float32).astype(jnp.bfloat16),
        "tensor",
        scatter_dimension=0,
        tiled=True,
    ).astype(jnp.float32)
    normed_ff = row_norm(middle, gain_f).astype(jnp.bfloat16)
    normed_ff_all = lax.all_gather(normed_ff, "tensor", axis=0, tiled=True)
    w_pair = jnp.concatenate([w_gate, w_up], axis=1)
    paired = jnp.dot(normed_ff_all, w_pair, preferred_element_type=jnp.float32)
    gate_values = paired[:, :ff_width]
    up_values = paired[:, ff_width:]
    hidden = geglu_mask(gate_values, up_values, keep_all[:, None]).astype(jnp.bfloat16)
    output = middle + lax.psum_scatter(
        jnp.dot(hidden, w_down, preferred_element_type=jnp.float32).astype(jnp.bfloat16),
        "tensor",
        scatter_dimension=0,
        tiled=True,
    ).astype(jnp.float32)
    activations = output.astype(jnp.bfloat16)
    cotangent = keep_mine[:, None] * (output - teacher.astype(jnp.float32))
    loss_part = jnp.sum(cotangent * cotangent)
    count_part = jnp.sum(keep_mine)
    shard_piece = lax.all_gather(cotangent.astype(jnp.bfloat16), "tensor", axis=0, tiled=True)
    grad_down_acc = lax.dot_general(
        hidden, shard_piece, contract_rows, preferred_element_type=jnp.float32
    )
    grad_rows = lax.dot_general(
        shard_piece, w_down, contract_cols, preferred_element_type=jnp.float32
    )
    grad_down = grad_down_acc
    grad_hidden = grad_rows
    _, geglu_back = jax.vjp(
        lambda gate_in, up_in: geglu_mask(gate_in, up_in, keep_all[:, None]), gate_values, up_values
    )
    grad_gate_rows, grad_up_rows = geglu_back(grad_hidden)
    grad_pair = jnp.concatenate([grad_gate_rows, grad_up_rows], axis=1).astype(jnp.bfloat16)
    grad_w_pair = lax.dot_general(
        normed_ff_all, grad_pair, contract_rows, preferred_element_type=jnp.float32
    )
    grad_normed_ff = lax.psum_scatter(
        lax.dot_general(
            grad_pair, w_pair, contract_cols, preferred_element_type=jnp.float32
        ).astype(jnp.bfloat16),
        "tensor",
        scatter_dimension=0,
        tiled=True,
    ).astype(jnp.float32)
    _, norm_back_ff = jax.vjp(row_norm, middle, gain_f)
    grad_middle_part, grad_gain_ff = norm_back_ff(grad_normed_ff)
    grad_middle = cotangent + grad_middle_part
    shard_piece = lax.all_gather(grad_middle.astype(jnp.bfloat16), "tensor", axis=0, tiled=True)
    grad_out_acc = lax.dot_general(
        mixed_parts, shard_piece, contract_rows, preferred_element_type=jnp.float32
    )
    grad_rows = lax.dot_general(
        shard_piece, w_out, contract_cols, preferred_element_type=jnp.float32
    )
    grad_out = grad_out_acc
    grad_mix = grad_rows.astype(jnp.bfloat16) * keep_all[:, None].astype(jnp.bfloat16)
    grad_bands = [jnp.zeros(bands.shape[1:], jnp.float32) for head in range(heads_here)]
    seq_index = 0
    low_row = seq_index * seq_len
    query_grads = []
    key_grads = []
    value_grads = []
    for head in range(heads_here):
        grad_head = grad_mix[low_row : low_row + seq_len, head * head_dim : (head + 1) * head_dim]
        grad_q, grad_k, grad_v, grad_bands[head] = attend_head_back(
            query_heads[head],
            key_heads[head],
            value_heads[head],
            grad_head,
            sums_parts[seq_index][head],
            lengths[seq_index],
            bands[head],
            grad_bands[head],
            block_rows,
            scale,
        )
        query_grads.append(grad_q)
        key_grads.append(grad_k.astype(jnp.bfloat16))
        value_grads.append(grad_v.astype(jnp.bfloat16))
    grad_parts = jnp.concatenate(query_grads + key_grads + value_grads, axis=1)
    _, bands_back = jax.vjp(lambda values: make_bands(values, block_rows, seq_len), relative)
    (grad_relative,) = bands_back(jnp.stack(grad_bands, axis=0))
    grad_w_joint = lax.dot_general(
        normed_all, grad_parts, contract_rows, preferred_element_type=jnp.float32
    )
    grad_table = lax.dot_general(one_hot, grad_relative, contract_table, precision=highest)
    grad_normed = lax.psum_scatter(
        lax.dot_general(
            grad_parts, w_joint, contract_cols, preferred_element_type=jnp.float32
        ).astype(jnp.bfloat16),
        "tensor",
        scatter_dimension=0,
        tiled=True,
    ).astype(jnp.float32)
    _, norm_back_attn = jax.vjp(row_norm, source, gain_a)
    grad_source_part, grad_gain_attn = norm_back_attn(grad_normed)
    grad_source = grad_middle + grad_source_part
    gain_attn_total, gain_ff_total, loss_total, count_total = lax.psum(
        (grad_gain_attn, grad_gain_ff, loss_part, count_part), ("dp", "tensor")
    )
    grad_w_joint, grad_out, grad_table, grad_w_pair, grad_down = lax.psum(
        (grad_w_joint, grad_out, grad_table, grad_w_pair, grad_down), "dp"
    )
    factor = 2.0 / (count_total * model_width)
    loss = loss_total / (count_total * model_width)
    return (
        activations,
        loss,
        grad_source * factor,
        gain_attn_total * factor,
        grad_w_joint[:, :local_width] * factor,
        grad_w_joint[:, local_width : 2 * local_width] * factor,
        grad_w_joint[:, 2 * local_width :] * factor,
        grad_out * factor,
        grad_table * factor,
        gain_ff_total * factor,
        grad_w_pair[:, :ff_width] * factor,
        grad_w_pair[:, ff_width:] * factor,
        grad_down * factor,
    )


def solution(mesh):
    in_specs = (
        P(("dp", "tensor"), None),
        P(("dp", "tensor"), None),
        P("dp"),
        P(),
        P(),
        P(None, "tensor"),
        P(None, "tensor"),
        P(None, "tensor"),
        P("tensor", None),
        P(None, "tensor"),
        P(),
        P(None, "tensor"),
        P(None, "tensor"),
        P("tensor", None),
    )
    out_specs = (
        P(("dp", "tensor"), None),
        P(),
        P(("dp", "tensor"), None),
        P(),
        P(None, "tensor"),
        P(None, "tensor"),
        P(None, "tensor"),
        P("tensor", None),
        P(None, "tensor"),
        P(),
        P(None, "tensor"),
        P(None, "tensor"),
        P("tensor", None),
    )
    return jax.shard_map(
        on_device, mesh=mesh, in_specs=in_specs, out_specs=out_specs, check_vma=False
    )
```

profile of v0, /device:TPU:0, one launch (start us, length us, event | category | flops | bytes accessed | tf_op | source)
XLA Modules:
  0.0 2142.2 jit_solution(9181588129690975066)
XLA Ops:
  22.2 24.8 %reshape.252 = f32[3938301]{0:T(1024)} reshape(f32[3,513,2559]{2,1,0:T(8,128)} %tile.40) | data formatting | bytes 31506408
  47.0 23.7 %tile.41 = f32[3,1312767]{1,0:T(4,128)} reshape(f32[3938301]{0:T(1024)} %reshape.252) | data formatting | bytes 31506408 | tf_op jit(solution)/shard_map/tile | solution.py:48
  92.3 44.7 %reshape.254 = f32[3929088]{0:T(1024)} reshape(f32[3,1309696]{1,0:T(4,128)} %slice.146) | data formatting | bytes 31432704
  137.0 24.7 %reshape.232 = f32[3,512,2558]{2,1,0:T(8,128)} reshape(f32[3929088]{0:T(1024)} %reshape.254) | data formatting | bytes 31432704 | tf_op jit(solution)/shard_map/reshape | solution.py:50
  169.2 23.9 %reshape.248 = f32[3938301]{0:T(1024)} reshape(f32[3,513,2559]{2,1,0:T(8,128)} %tile.42) | data formatting | bytes 31506408
  193.1 23.7 %tile.43 = f32[3,1312767]{1,0:T(4,128)} reshape(f32[3938301]{0:T(1024)} %reshape.248) | data formatting | bytes 31506408 | tf_op jit(solution)/shard_map/tile | solution.py:48
  238.7 44.4 %reshape.250 = f32[3929088]{0:T(1024)} reshape(f32[3,1309696]{1,0:T(4,128)} %slice.149) | data formatting | bytes 31432704
  283.1 24.8 %reshape.233 = f32[3,512,2558]{2,1,0:T(8,128)} reshape(f32[3929088]{0:T(1024)} %reshape.250) | data formatting | bytes 31432704 | tf_op jit(solution)/shard_map/reshape | solution.py:50
  315.4 24.2 %reshape.260 = f32[3938301]{0:T(1024)} reshape(f32[3,513,2559]{2,1,0:T(8,128)} %tile.16) | data formatting | bytes 31506408
  339.6 23.7 %tile.17 = f32[3,1312767]{1,0:T(4,128)} reshape(f32[3938301]{0:T(1024)} %reshape.260) | data formatting | bytes 31506408 | tf_op jit(solution)/shard_map/tile | solution.py:48
  384.9 44.7 %reshape.262 = f32[3929088]{0:T(1024)} reshape(f32[3,1309696]{1,0:T(4,128)} %slice.140) | data formatting | bytes 31432704
  429.6 24.8 %reshape.230 = f32[3,512,2558]{2,1,0:T(8,128)} reshape(f32[3929088]{0:T(1024)} %reshape.262) | data formatting | bytes 31432704 | tf_op jit(solution)/shard_map/reshape | solution.py:50
  461.9 23.9 %reshape.256 = f32[3938301]{0:T(1024)} reshape(f32[3,513,2559]{2,1,0:T(8,128)} %tile.18) | data formatting | bytes 31506408
  485.8 23.7 %tile.19 = f32[3,1312767]{1,0:T(4,128)} reshape(f32[3938301]{0:T(1024)} %reshape.256) | data formatting | bytes 31506408 | tf_op jit(solution)/shard_map/tile | solution.py:48
  531.2 44.9 %reshape.258 = f32[3929088]{0:T(1024)} reshape(f32[3,1309696]{1,0:T(4,128)} %slice.143) | data formatting | bytes 31432704
  576.1 24.8 %reshape.231 = f32[3,512,2558]{2,1,0:T(8,128)} reshape(f32[3929088]{0:T(1024)} %reshape.258) | data formatting | bytes 31432704 | tf_op jit(solution)/shard_map/reshape | solution.py:50
  635.4 34.5 %pad_maximum_fusion = f32[3,4,512,2048]{3,2,1,0:T(8,128)} fusion(f32[3,1,512,2048]{3,2,1,0:T(8,128)} %get-tuple-element.1597, f32[3,1,512,2048]{3,2,1,0:T(8,128)} %get-tuple-element.1598, f32[3,1,512,2048]{3,2,1,0:T(8,128)} %get-tuple-element.1599, f32[3,1,512,2048]{3,2,1,0:T(8,128)} %get-tuple-element.1600), kind=kLoop, calls=%fused_computation.120 | loop fusion | flops 37748736 | bytes 100663296 | tf_op jit(solution)/shard_map/stack | solution.py:60
  669.9 33.4 %slice_bitcast_fusion = (f32[4,512,2048]{2,1,0:T(8,128)}, f32[4,512,2048]{2,1,0:T(8,128)}, f32[4,512,2048]{2,1,0:T(8,128)}) fusion(f32[3,4,512,2048]{3,2,1,0:T(8,128)} %pad_maximum_fusion), kind=kLoop, calls=%fused_computation.122 | loop fusion | bytes 100663296 | tf_op jit(solution)/shard_map/squeeze | solution.py:214
  715.2 30.8 %while.109 = (s32[]{:T(128)}, bf16[2048,64]{0,1:T(8,128)(2,1)}, f32[2048]{0:T(1024)}, bf16[2048,64]{1,0:T(8,128)(2,1)}, bf16[2048,64]{1,0:T(8,128)(2,1)S(1)}, /*...) while((s32[]{:T(128)}, bf16[2048,64]{0,1:T(8,128)(2,1)}, ...), condition=%wide.region_8.9_spmd.clone, body=%wide.region_5.8_spmd.clone.sunk | while | flops 277939712 | bytes 17525440 | solution.py:90
  756.8 23.2 %while.108 = (s32[]{:T(128)}, bf16[2048,64]{0,1:T(8,128)(2,1)S(1)}, f32[2048]{0:T(1024)S(1)}, bf16[2048,64]{1,0:T(8,128)(2,1)}, bf16[2048,64]{1,0:T(8,128)(2,1)S...) while((s32[]{:T(128)}, bf16[2048,64]{0,1:T(8,128)(2,1)S(1)}, ...), condition=%wide.region_4.5_spmd.clone, body=%wide.region_1.4_spmd.clone.sunk | while | flops 277939712 | bytes 17787584 | solution.py:90
  792.2 27.5 %while.110 = (s32[]{:T(128)}, bf16[2048,64]{0,1:T(8,128)(2,1)S(1)}, f32[2048]{0:T(1024)S(1)}, bf16[2048,64]{1,0:T(8,128)(2,1)}, bf16[2048,64]{1,0:T(8,128)(2,1)S...) while((s32[]{:T(128)}, bf16[2048,64]{0,1:T(8,128)(2,1)S(1)}, ...), condition=%wide.region_12.13_spmd.clone, body=%wide.region_9.12_spmd.clone.sunk | while | flops 277939712 | bytes 17525440 | solution.py:90
  824.7 40.7 %reduce-scatter.5.cloned.1.call-done = bf16[512,768]{1,0:T(8,128)(2,1)} async-done(((bf16[2048,768]{1,0:T(8,128)(2,1)}), bf16[512,768]{1,0:T(8,128)(2,1)}) %reduce-scatter.5.cloned.1.call-update) | async-done | bytes 786448 | tf_op jit(solution)/shard_map/reduce_scatter | solution.py:222
  872.4 25.6 %all-gather.7.cloned.1.call-done = bf16[2048,768]{1,0:T(8,128)(2,1)} async-done(((bf16[512,768]{1,0:T(8,128)(2,1)}), bf16[2048,768]{1,0:T(8,128)(2,1)}) %all-gather.7.cloned.1.call-update) | async-done | bytes 3145744 | tf_op jit(solution)/shard_map/all_gather | solution.py:229
  912.2 38.0 %reduce-scatter.7.cloned.1.call-done = bf16[512,768]{1,0:T(8,128)(2,1)} async-done(((bf16[2048,768]{1,0:T(8,128)(2,1)}), bf16[512,768]{1,0:T(8,128)(2,1)}) %reduce-scatter.7.cloned.1.call-update) | async-done | bytes 786448 | tf_op jit(solution)/shard_map/reduce_scatter | solution.py:235
  953.0 28.6 %all-gather.9.cloned.1.call-done = bf16[2048,768]{1,0:T(8,128)(2,1)} async-done(((bf16[512,768]{1,0:T(8,128)(2,1)}), bf16[2048,768]{1,0:T(8,128)(2,1)}) %all-gather.9.cloned.1.call-update) | async-done | bytes 3145744 | tf_op jit(solution)/shard_map/all_gather | solution.py:245
  998.3 38.1 %reduce-scatter.9.cloned.1.call-done = bf16[512,768]{1,0:T(8,128)(2,1)} async-done(((bf16[2048,768]{1,0:T(8,128)(2,1)}), bf16[512,768]{1,0:T(8,128)(2,1)}) %reduce-scatter.9.cloned.1.call-update) | async-done | bytes 786448 | tf_op jit(solution)/shard_map/reduce_scatter | solution.py:262
  1041.6 28.6 %all-gather.11.cloned.1.call-done = bf16[2048,768]{1,0:T(8,128)(2,1)} async-done(((bf16[512,768]{1,0:T(8,128)(2,1)}), bf16[2048,768]{1,0:T(8,128)(2,1)}) %all-gather.11.cloned.1.call-update) | async-done | bytes 3145744 | tf_op jit(solution)/shard_map/all_gather | solution.py:273
  1082.7 76.9 %while.113 = (s32[]{:T(128)}, bf16[2048,64]{0,1:T(8,128)(2,1)}, f32[2048,64]{0,1:T(8,128)}, f32[2048,64]{0,1:T(8,128)S(1)}, f32[4,512,2048]{2,1,0:T(8,128)}, /*i...) while((s32[]{:T(128)}, bf16[2048,64]{0,1:T(8,128)(2,1)}, ...), condition=%wide.region_30.31_spmd.clone, body=%wide.region_28.30_spmd.clone.sunk | while | flops 684393984 | bytes 81214752 | solution.py:156
  1169.0 82.1 %while.112 = (s32[]{:T(128)}, bf16[2048,64]{0,1:T(8,128)(2,1)}, f32[2048,64]{0,1:T(8,128)}, f32[2048,64]{0,1:T(8,128)}, f32[4,512,2048]{2,1,0:T(8,128)}, /*index...) while((s32[]{:T(128)}, bf16[2048,64]{0,1:T(8,128)(2,1)}, ...), condition=%wide.region_27.28_spmd.clone, body=%wide.region_25.27_spmd.clone.sunk | while | flops 684393984 | bytes 80952608 | solution.py:156
  1259.9 77.5 %while.111 = (s32[]{:T(128)}, bf16[2048,64]{0,1:T(8,128)(2,1)}, f32[2048,64]{0,1:T(8,128)}, f32[2048,64]{0,1:T(8,128)}, f32[4,512,2048]{2,1,0:T(8,128)}, /*index...) while((s32[]{:T(128)}, bf16[2048,64]{0,1:T(8,128)(2,1)}, ...), condition=%wide.region_24.25_spmd.clone, body=%wide.region_22.24_spmd.clone.sunk | while | flops 684393984 | bytes 81214752 | solution.py:156
  1367.8 35.1 %pad_maximum_fusion.1 = f32[3,4,512,2048]{3,2,1,0:T(8,128)} fusion(f32[1,4,512,2048]{3,2,1,0:T(8,128)} %bitcast.176, f32[1,4,512,2048]{3,2,1,0:T(8,128)} %bitcast.177, f32[1,4,512,2048]{3,2,1,0:T(8,128)} %bitcast.175), kind=kLoop, calls=%fused_computation.121 | loop fusion | flops 25165824 | bytes 100663296 | tf_op jit(solution)/shard_map/stack | solution.py:307
  1402.9 32.0 %slice_bitcast_fusion.6 = (f32[3,512,2048]{2,1,0:T(8,128)}, f32[3,512,2048]{2,1,0:T(8,128)}, f32[3,512,2048]{2,1,0:T(8,128)}, f32[3,512,2048]{2,1,0:T(8,128)}) fusion(f32[3,4,512,2048]{3,2,1,0:T(8,128)} %pad_maximum_fusion.1), kind=kLoop, calls=%fused_computation.128 | loop fusion | bytes 100663296 | tf_op jit(solution)/shard_map/transpose(jvp())/unstack | solution.py:60
  1447.3 25.3 %reshape.276 = f32[3929088]{0:T(1024)} reshape(f32[3,512,2558]{2,1,0:T(8,128)} %pad.36) | data formatting | bytes 31432704
  1472.6 23.1 %reshape.234 = f32[3,1309696]{1,0:T(4,128)} reshape(f32[3929088]{0:T(1024)} %reshape.276) | data formatting | bytes 31432704 | tf_op jit(solution)/shard_map/transpose(jvp())/reshape | solution.py:50
  1512.5 47.8 %reshape.278 = f32[3938301]{0:T(1024)} reshape(f32[3,1312767]{1,0:T(4,128)} %pad.37) | data formatting | bytes 31506408
  1560.3 26.1 %reshape.235 = f32[3,513,2559]{2,1,0:T(8,128)} reshape(f32[3938301]{0:T(1024)} %reshape.278) | data formatting | bytes 31506408 | tf_op jit(solution)/shard_map/transpose(jvp())/reshape | solution.py:48
  1598.7 25.4 %reshape.272 = f32[3929088]{0:T(1024)} reshape(f32[3,512,2558]{2,1,0:T(8,128)} %pad.39) | data formatting | bytes 31432704
  1624.2 22.5 %reshape.236 = f32[3,1309696]{1,0:T(4,128)} reshape(f32[3929088]{0:T(1024)} %reshape.272) | data formatting | bytes 31432704 | tf_op jit(solution)/shard_map/transpose(jvp())/reshape | solution.py:50
  1663.6 46.3 %reshape.274 = f32[3938301]{0:T(1024)} reshape(f32[3,1312767]{1,0:T(4,128)} %pad.40) | data formatting | bytes 31506408
  1709.9 25.7 %reshape.237 = f32[3,513,2559]{2,1,0:T(8,128)} reshape(f32[3938301]{0:T(1024)} %reshape.274) | data formatting | bytes 31506408 | tf_op jit(solution)/shard_map/transpose(jvp())/reshape | solution.py:48
  1747.6 25.6 %reshape.268 = f32[3929088]{0:T(1024)} reshape(f32[3,512,2558]{2,1,0:T(8,128)} %pad.42) | data formatting | bytes 31432704
  1773.2 22.5 %reshape.238 = f32[3,1309696]{1,0:T(4,128)} reshape(f32[3929088]{0:T(1024)} %reshape.268) | data formatting | bytes 31432704 | tf_op jit(solution)/shard_map/transpose(jvp())/reshape | solution.py:50
  1812.4 46.3 %reshape.270 = f32[3938301]{0:T(1024)} reshape(f32[3,1312767]{1,0:T(4,128)} %pad.43) | data formatting | bytes 31506408
  1858.7 25.9 %reshape.239 = f32[3,513,2559]{2,1,0:T(8,128)} reshape(f32[3938301]{0:T(1024)} %reshape.270) | data formatting | bytes 31506408 | tf_op jit(solution)/shard_map/transpose(jvp())/reshape | solution.py:48
  1896.6 25.2 %reshape.264 = f32[3929088]{0:T(1024)} reshape(f32[3,512,2558]{2,1,0:T(8,128)} %pad.45) | data formatting | bytes 31432704
  1961.1 46.5 %reshape.266 = f32[3938301]{0:T(1024)} reshape(f32[3,1312767]{1,0:T(4,128)} %pad.46) | data formatting | bytes 31506408
  2007.6 25.6 %reshape.241 = f32[3,513,2559]{2,1,0:T(8,128)} reshape(f32[3938301]{0:T(1024)} %reshape.266) | data formatting | bytes 31506408 | tf_op jit(solution)/shard_map/transpose(jvp())/reshape | solution.py:48
  2083.3 37.3 %all-reduce.12 = (f32[]{:T(128)}, f32[]{:T(128)}, f32[768]{0:T(1024)S(1)}, f32[768]{0:T(1024)S(1)}) all-reduce(f32[]{:T(128)} %get-tuple-element.1419, f32[]{:T(128)} %fusion.150, f32[768]{0:T(1024)S(1)} %get-tuple-element.1420, f32[768]{0:T(1024)S(1)} %copy-done.64), channel_id=1, replica_groups=mesh['dp'=8,'tensor'=4] {'dp','tensor'}, use_global_device_ids=true, to_apply=%region_17.18 | all-reduce | flops 1538 | bytes 12304 | tf_op jit(solution)/shard_map/psum | solution.py:323
  (485 shorter events, 821.3 us)
Async XLA Ops:
  7.2 901.4 %copy-start = (bf16[512,768]{1,0:T(8,128)(2,1)S(1)}, bf16[512,768]{1,0:T(8,128)(2,1)}, u32[]{:S(2)}) copy-start(bf16[512,768]{1,0:T(8,128)(2,1)} %param.39) | copy-start | bytes 2359300
  7.2 696.2 %all-gather.5.cloned.1.call-start = ((), (), s32[]{:S(2)}) async-start(), calls=%async_computation.4 | async-start | bytes 3932160 | tf_op jit(solution)/shard_map/all_gather | solution.py:194
  12.8 852.7 %reduce-scatter.5.cloned.1.call-start = ((), (), s32[]{:S(2)}) async-start(), calls=%async_computation.5 | async-start | bytes 3932160 | tf_op jit(solution)/shard_map/reduce_scatter | solution.py:222
  429.6 24.8 %copy-start.46 = (f32[3,2559]{1,0:T(4,128)S(1)}, f32[3,2559]{1,0:T(4,128)}, u32[]{:S(2)}) copy-start(f32[3,2559]{1,0:T(4,128)} %get-tuple-element.1596) | copy-start | bytes 92128
  600.9 21.3 copy-start.15
  669.9 33.4 %copy-start.39 = (bf16[768,192]{0,1:T(8,128)(2,1)S(1)}, bf16[768,192]{0,1:T(8,128)(2,1)}, u32[]{:S(2)}) copy-start(bf16[768,192]{0,1:T(8,128)(2,1)} %param.31) | copy-start | bytes 884740
  820.7 44.8 %copy-start.13 = (bf16[512,768]{1,0:T(8,128)(2,1)S(1)}, bf16[512,768]{1,0:T(8,128)(2,1)}, u32[]{:S(2)}) copy-start(bf16[512,768]{1,0:T(8,128)(2,1)} %param.26) | copy-start | bytes 2359300
  824.7 73.3 %all-gather.7.cloned.1.call-start = ((), (), s32[]{:S(2)}) async-start(), calls=%async_computation.6 | async-start | bytes 3932160 | tf_op jit(solution)/shard_map/all_gather | solution.py:229
  824.7 44.6 %copy-start.37 = (bf16[768,512]{1,0:T(8,128)(2,1)S(1)}, bf16[768,512]{1,0:T(8,128)(2,1)}, u32[]{:S(2)}) copy-start(bf16[768,512]{1,0:T(8,128)(2,1)} %param.37) | copy-start | bytes 2359300
  824.7 214.9 %copy-start.47 = (f32[768]{0:T(1024)}, f32[768]{0:T(1024)S(1)}, u32[]{:S(2)}) copy-start(f32[768]{0:T(1024)S(1)} %convert_element_type.265) | copy-start | bytes 9220
  867.0 172.7 %copy-start.53 = (f32[512]{0:T(512)}, f32[512]{0:T(512)S(1)}, u32[]{:S(2)}) copy-start(f32[512]{0:T(512)S(1)} %fusion.149) | copy-start | bytes 6148
  869.3 80.9 %reduce-scatter.7.cloned.1.call-start = ((), (), s32[]{:S(2)}) async-start(), calls=%async_computation.7 | async-start | bytes 3932160 | tf_op jit(solution)/shard_map/reduce_scatter | solution.py:235
  908.6 41.7 %copy-start.16 = (bf16[512,768]{1,0:T(8,128)(2,1)S(1)}, bf16[512,768]{1,0:T(8,128)(2,1)}, u32[]{:S(2)}) copy-start(bf16[512,768]{1,0:T(8,128)(2,1)} %reduce-scatter.5.cloned.1.call-done) | copy-start | bytes 2359300
  912.1 69.5 %all-gather.9.cloned.1.call-start = ((), (), s32[]{:S(2)}) async-start(), calls=%async_computation.8 | async-start | bytes 3932160 | tf_op jit(solution)/shard_map/all_gather | solution.py:245
  912.2 127.5 %copy-start.51 = (f32[512]{0:T(512)}, f32[512]{0:T(512)S(1)}, u32[]{:S(2)}) copy-start(f32[512]{0:T(512)S(1)} %fusion.147) | copy-start | bytes 6148
  952.9 83.4 %reduce-scatter.9.cloned.1.call-start = ((), (), s32[]{:S(2)}) async-start(), calls=%async_computation.9 | async-start | bytes 3932160 | tf_op jit(solution)/shard_map/reduce_scatter | solution.py:262
  991.8 44.6 %copy-start.24 = (bf16[512,768]{1,0:T(8,128)(2,1)S(1)}, bf16[512,768]{1,0:T(8,128)(2,1)}, u32[]{:S(2)}) copy-start(bf16[512,768]{1,0:T(8,128)(2,1)} %param.27) | copy-start | bytes 2359300
  998.2 71.9 %copy-start.45 = (bf16[192,768]{1,0:T(8,128)(2,1)S(1)}, bf16[192,768]{1,0:T(8,128)(2,1)}, u32[]{:S(2)}) copy-start(bf16[192,768]{1,0:T(8,128)(2,1)} %param.34) | copy-start | bytes 884740
  998.2 71.9 %all-gather.11.cloned.1.call-start = ((), (), s32[]{:S(2)}) async-start(), calls=%async_computation.10 | async-start | bytes 3932160 | tf_op jit(solution)/shard_map/all_gather | solution.py:273
  1039.7 33.5 %copy-start.62 = (f32[512]{0:T(512)}, f32[512]{0:T(512)S(1)}, u32[]{:S(2)}) copy-start(f32[512]{0:T(512)S(1)} %multiply_multiply_fusion.4) | copy-start | bytes 6148
  1041.4 1039.9 %reduce-scatter.11.cloned.1.call-start = ((), (), s32[]{:S(2)}) async-start(), calls=%async_computation.11 | async-start | bytes 3932160 | tf_op jit(solution)/shard_map/reduce_scatter | solution.py:312
  1108.3 7.4 copy-start.2
  1146.8 7.3 copy-start.2
  1160.3 8.7 copy-start.12
  1160.3 8.7 copy-start.21
  1175.9 7.3 copy-start.4
  1216.6 7.4 copy-start.4
  1237.2 7.3 copy-start.4
  1251.1 8.7 copy-start.10
  1251.1 8.7 copy-start.19
  1304.0 7.4 copy-start.6
  1337.4 8.4 copy-start.23
  1337.4 9.9 copy-start.40
  1337.4 9.9 copy-start.42
  1337.4 9.9 copy-start.44
  1351.4 775.9 %all-reduce.16.cloned.1.call-start = ((), (), s32[]{:S(2)}) async-start(), calls=%async_computation.12 | async-start | bytes 14155776 | tf_op jit(solution)/shard_map/psum | solution.py:326
  2052.5 28.9 %copy-start.14 = (bf16[512,768]{1,0:T(8,128)(2,1)S(1)}, bf16[512,768]{1,0:T(8,128)(2,1)}, u32[]{:S(2)}) copy-start(bf16[512,768]{1,0:T(8,128)(2,1)} %param.26) | copy-start | bytes 2359300
  2052.5 28.9 %copy-start.50 = (f32[768]{0:T(1024)S(1)}, f32[768]{0:T(1024)}, u32[]{:S(2)}) copy-start(f32[768]{0:T(1024)} %copy-done.49) | copy-start | bytes 9220
  2052.5 28.9 %copy-start.57 = (f32[512]{0:T(512)S(1)}, f32[512]{0:T(512)}, u32[]{:S(2)}) copy-start(f32[512]{0:T(512)} %copy-done.56) | copy-start | bytes 6148
  2052.5 30.8 %copy-start.64 = (f32[768]{0:T(1024)S(1)}, f32[768]{0:T(1024)}, u32[]{:S(2)}) copy-start(f32[768]{0:T(1024)} %get-tuple-element.1417) | copy-start | bytes 9220
  2052.5 70.0 %copy-start.61 = (f32[512]{0:T(512)S(1)}, f32[512]{0:T(512)}, u32[]{:S(2)}) copy-start(f32[512]{0:T(512)} %copy-done.60) | copy-start | bytes 6148
  2052.5 71.2 %copy-start.17 = (bf16[512,768]{1,0:T(8,128)(2,1)S(1)}, bf16[512,768]{1,0:T(8,128)(2,1)}, u32[]{:S(2)}) copy-start(bf16[512,768]{1,0:T(8,128)(2,1)} %reduce-scatter.5.cloned.1.call-done) | copy-start | bytes 2359300
  2052.6 71.2 %copy-start.25 = (bf16[512,768]{1,0:T(8,128)(2,1)S(1)}, bf16[512,768]{1,0:T(8,128)(2,1)}, u32[]{:S(2)}) copy-start(bf16[512,768]{1,0:T(8,128)(2,1)} %param.27) | copy-start | bytes 2359300
  2052.6 71.2 %copy-start.27 = (bf16[512,768]{1,0:T(8,128)(2,1)S(1)}, bf16[512,768]{1,0:T(8,128)(2,1)}, u32[]{:S(2)}) copy-start(bf16[512,768]{1,0:T(8,128)(2,1)} %reduce-scatter.7.cloned.1.call-done) | copy-start | bytes 2359300
  2052.6 71.2 %copy-start.48 = (f32[768]{0:T(1024)S(1)}, f32[768]{0:T(1024)}, u32[]{:S(2)}) copy-start(f32[768]{0:T(1024)} %copy-done.47) | copy-start | bytes 9220
  2052.6 71.2 %copy-start.52 = (f32[512]{0:T(512)S(1)}, f32[512]{0:T(512)}, u32[]{:S(2)}) copy-start(f32[512]{0:T(512)} %copy-done.51) | copy-start | bytes 6148
  2052.6 71.2 %copy-start.54 = (f32[512]{0:T(512)S(1)}, f32[512]{0:T(512)}, u32[]{:S(2)}) copy-start(f32[512]{0:T(512)} %copy-done.53) | copy-start | bytes 6148
  2052.6 71.2 %copy-start.63 = (f32[512]{0:T(512)S(1)}, f32[512]{0:T(512)}, u32[]{:S(2)}) copy-start(f32[512]{0:T(512)} %copy-done.62) | copy-start | bytes 6148
  (51 other events, 213.0 us)
Sparse Core Ops, SparseCore 0:
  12.9 31.2 all-gather.4
  824.8 40.6 reduce-scatter.4
  869.4 28.5 all-gather.6
  912.2 37.9 reduce-scatter.6
  953.1 28.5 all-gather.8
  998.3 37.9 reduce-scatter.8
  1041.6 28.5 all-gather.10
  1351.5 37.9 reduce-scatter.10
  1395.1 235.8 all-reduce.15
where the time goes:
time: 2160 us; the launch traced here: 2140 us
  local copies, waits for them, and re-layouts  1340 us (62%)
  matrix products  269 us (12%)
  other arithmetic  252 us (12%)
  waiting for transfers between devices  200 us (9%)
  blocking collectives  58.8 us (3%)
    unnamed x163, local copies, waits for them, and re-layouts  586 us
    reshape x8, local copies, waits for them, and re-layouts, band_matrix(): return tiled.reshape(heads_here, block_rows, span - 1)[:, :, :seq_len]  190 us
    another operation x8, local copies, waits for them, and re-layouts, band_matrix(): tiled = jnp.tile(window, (1, block_rows + 1))  125 us
    reshape x4, local copies, waits for them, and re-layouts, band_matrix(): tiled = jnp.tile(window, (1, block_rows + 1))  103 us
    dynamic_update_slice x12, other arithmetic, one_block(): lax.dynamic_update_slice_in_dim(grad_band, current + grad_scores.astype(j...  88.1 us
    slice x4, local copies, waits for them, and re-layouts, band_matrix(): tiled = tiled[:, block_rows - 1:block_rows - 1 + block_rows * (span - 1)]  86.6 us
    dot_general x24, matrix products, one_block(): lax.dot_general(query_block, key_head, contract_cols, preferred_element_t...  84 us
    pad x4, local copies, waits for them, and re-layouts, band_matrix(): tiled = tiled[:, block_rows - 1:block_rows - 1 + block_rows * (span - 1)]  67 us
  transfers between devices with their start and end apart: 9, of which 6 were waited for; matrix products, arithmetic and copies ran while one was open for 66% of the time, Pallas kernels for 0%

commit v1 on v0

v1 whole, which is shorter than its diff:
```python
import jax
import jax.numpy as jnp
from jax import lax
from jax.experimental import pallas as pl
from jax.experimental.pallas import tpu as pltpu
from jax.sharding import PartitionSpec as P

F32, BF16 = jnp.float32, jnp.bfloat16
QB = 256
KC = 256

eps_norm = 1e-06
masked_score = -1e30
highest = lax.Precision.HIGHEST
contract_rows = (((0,), (0,)), ((), ()))
contract_cols = (((1,), (1,)), ((), ()))
contract_table = (((0,), (1,)), ((), ()))


def row_norm(values, gain):
    inverse = lax.rsqrt(jnp.mean(values * values, axis=-1, keepdims=True) + eps_norm)
    return values * inverse * gain


def geglu_mask(gate_values, up_values, keep_column):
    return keep_column * jax.nn.gelu(gate_values, approximate=True) * up_values


def valid_mask(lengths, first_row, row_count, seq_len):
    positions = first_row + lax.iota(jnp.int32, row_count)
    owners = positions // seq_len
    within = positions % seq_len
    chosen = owners[:, None] == lax.iota(jnp.int32, lengths.shape[0])[None, :]
    limits = jnp.sum(jnp.where(chosen, lengths[None, :], 0), axis=1)
    return (within < limits).astype(jnp.float32)


def bucket_rows(buckets, bias_table):
    one_hot = (buckets[:, None] == lax.iota(jnp.int32, bias_table.shape[0])[None, :]).astype(
        jnp.float32
    )
    relative = lax.dot_general(
        bias_table.astype(jnp.float32), one_hot, contract_table, precision=highest
    )
    return (one_hot, relative)


NT = (((1,), (1,)), ((), ()))
TN = (((0,), (0,)), ((), ()))
NN = (((1,), (0,)), ((), ()))

def dot(a, b, dims=NN):
    return lax.dot_general(a, b, dims, preferred_element_type=F32)

def split3(v):
    hi = v.astype(BF16); r = v - hi.astype(F32)
    mid = r.astype(BF16); r = r - mid.astype(F32)
    return hi, mid, r.astype(BF16)

def fill_band(band, row):
    rows, span = band.shape
    base = pltpu.roll(jnp.broadcast_to(row, (8, span)), 0, 1, stride=1, stride_axis=0)
    for g in range(rows // 8):
        band[8 * g:8 * g + 8, :] = pltpu.roll(base, 8 * g, 1) if g else base

def fwd_kernel(len_ref, rel_ref, qkv_ref, mixed_ref, qa_ref, ka_ref, va_ref, band):
    head = pl.program_id(0)
    heads = pl.num_programs(0)
    seq = qkv_ref.shape[0]
    nheads = mixed_ref.shape[1] // 64
    hd = 64
    local = nheads * hd
    length = len_ref[0]
    lane = lax.broadcasted_iota(jnp.int32, (seq, 128), 1)
    row = lax.broadcasted_iota(jnp.int32, (seq, 128), 0)
    for h in range(nheads):
        @pl.when(head == h)
        def _():
            pad = jnp.zeros((seq, 64), BF16)
            q = qkv_ref[:, h * hd:(h + 1) * hd] * jnp.asarray(hd ** -0.5, BF16)
            k = qkv_ref[:, local + h * hd:local + (h + 1) * hd]
            v = qkv_ref[:, 2 * local + h * hd:2 * local + (h + 1) * hd]
            one = jnp.ones((), BF16)
            qa_ref[0] = jnp.where(lane == 67, one, jnp.concatenate([q, pad], axis=1))
            kx = jnp.where((lane >= 64) & (lane < 67), one, jnp.concatenate([k, pad], axis=1))
            ka_ref[0] = jnp.where((lane == 67) & (row >= length), jnp.asarray(-1e30, BF16), kx)
            va_ref[0] = jnp.where((lane >= 64) & (lane < 67), one, jnp.concatenate([v, pad], axis=1))
    fill_band(band, rel_ref[0])
    blane = lax.broadcasted_iota(jnp.int32, (QB, 128), 1)

    def block(step, carry):
        q0 = pl.multiple_of(step * QB, QB)
        q = qa_ref[0, pl.ds(q0, QB), :]
        start = pl.multiple_of(seq - q0, QB)
        s = dot(q, ka_ref[0], NT) + band[:, pl.ds(start, seq)]
        m = jnp.max(s, axis=1, keepdims=True)
        p = jnp.exp(s - m)
        total = jnp.sum(p, axis=1, keepdims=True)
        o = dot(p.astype(BF16), va_ref[0])
        rows = q0 + lax.broadcasted_iota(jnp.int32, (QB, 1), 0)
        keep = (rows < length).astype(F32)
        o = (o[:, :hd] * (keep / total)).astype(BF16)
        for h in range(nheads):
            @pl.when(head == h)
            def _():
                mixed_ref[pl.ds(q0, QB), h * hd:(h + 1) * hd] = o
        lse = -(m + jnp.log(total))
        hi, mid, lo = split3(lse)
        qa_ref[0, pl.ds(q0, QB), :] = jnp.where(blane == 64, hi, jnp.where(blane == 65, mid, jnp.where(blane == 66, lo, q)))
        return carry
    lax.fori_loop(0, seq // QB, block, 0)

def attend(length, rel, qkv, heads):
    seq = qkv.shape[0]
    span = rel.shape[-1]
    aug = jax.ShapeDtypeStruct((heads, seq, 128), BF16)
    aspec = pl.BlockSpec((1, seq, 128), lambda h: (h, 0, 0))
    return pl.pallas_call(
        fwd_kernel, grid=(heads,),
        out_shape=(jax.ShapeDtypeStruct((seq, heads * 64), BF16), aug, aug, aug),
        in_specs=[pl.BlockSpec(memory_space=pltpu.SMEM), pl.BlockSpec((1, 1, span), lambda h: (h, 0, 0)),
                  pl.BlockSpec((seq, 3 * heads * 64), lambda h: (0, 0))],
        out_specs=(pl.BlockSpec((seq, heads * 64), lambda h: (0, 0)), aspec, aspec, aspec),
        scratch_shapes=[pltpu.VMEM((QB, span), F32)],
        compiler_params=pltpu.CompilerParams(vmem_limit_bytes=56 << 20),
        name="attend_fwd",
    )(length, rel.reshape(heads, 1, span), qkv)

def bwd_kernel(rev_ref, dmix_ref, mixed_ref, qa_ref, ka_ref, va_ref, grads_ref, grev_ref, band, gband, da, kt, dq):
    head = pl.program_id(0)
    seq = qa_ref.shape[1]
    hd = 64
    nheads = mixed_ref.shape[1] // hd
    local = nheads * hd
    lane = lax.broadcasted_iota(jnp.int32, (seq, 128), 1)
    for h in range(nheads):
        @pl.when(head == h)
        def _():
            g = dmix_ref[:, h * hd:(h + 1) * hd]
            o = mixed_ref[:, h * hd:(h + 1) * hd]
            inner = -jnp.sum(g.astype(F32) * o.astype(F32), axis=1, keepdims=True)
            hi, mid, lo = split3(inner)
            gx = jnp.concatenate([g, jnp.zeros((seq, 64), BF16)], axis=1)
            da[...] = jnp.where(lane == 64, hi, jnp.where(lane == 65, mid, jnp.where(lane == 66, lo, gx)))
    kt[...] = ka_ref[0].astype(F32).T.astype(BF16)
    fill_band(band, rev_ref[0])
    gband[...] = jnp.zeros_like(gband)
    dq[...] = jnp.zeros_like(dq)

    def block(step, carry):
        k0 = pl.multiple_of(step * QB, QB)
        k = ka_ref[0, pl.ds(k0, QB), :]
        v = va_ref[0, pl.ds(k0, QB), :]
        ktb = kt[:, pl.ds(k0, QB)]
        dv = jnp.zeros((QB, 128), F32)
        dk = jnp.zeros((QB, 128), F32)
        for c in range(seq // KC):
            cols = slice(c * KC, (c + 1) * KC)
            off = pl.ds(pl.multiple_of(seq - k0 + c * KC, KC), KC)
            qc = qa_ref[0, cols, :]
            dc = da[cols, :]
            p = jnp.exp(dot(k, qc, NT) + band[:, off])
            ds = p * dot(v, dc, NT)
            gband[:, off] += ds
            pb = p.astype(BF16)
            db = ds.astype(BF16)
            dv += dot(pb, dc)
            dk += dot(db, qc)
            dq[:, cols] += dot(ktb, db)
        for h in range(nheads):
            @pl.when(head == h)
            def _():
                grads_ref[pl.ds(k0, QB), local + h * hd:local + (h + 1) * hd] = dk[:, :hd].astype(BF16)
                grads_ref[pl.ds(k0, QB), 2 * local + h * hd:2 * local + (h + 1) * hd] = dv[:, :hd].astype(BF16)
        return carry
    lax.fori_loop(0, seq // QB, block, 0)
    for h in range(nheads):
        @pl.when(head == h)
        def _():
            dqt = (dq[...] * (hd ** -0.5)).T
            grads_ref[:, h * hd:(h + 1) * hd] = dqt[:, :hd].astype(BF16)
    span = gband.shape[1]
    acc = gband[0:8, :]
    for g in range(1, QB // 8):
        acc = acc + pltpu.roll(gband[8 * g:8 * g + 8, :], span - 8 * g, 1)
    sub = lax.broadcasted_iota(jnp.int32, (8, span), 0)
    for bit in (1, 2, 4):
        acc = jnp.where((sub & bit) != 0, pltpu.roll(acc, span - bit, 1), acc)
    grev_ref[0] = jnp.sum(acc, axis=0, keepdims=True)

def attend_back(rev, dmix, mixed, qa, ka, va):
    heads, seq, _ = qa.shape
    span = rev.shape[-1]
    aspec = pl.BlockSpec((1, seq, 128), lambda h: (h, 0, 0))
    whole = lambda w: pl.BlockSpec((seq, w), lambda h: (0, 0))
    rspec = pl.BlockSpec((1, 1, span), lambda h: (h, 0, 0))
    grads, grev = pl.pallas_call(
        bwd_kernel, grid=(heads,),
        out_shape=(jax.ShapeDtypeStruct((seq, 3 * heads * 64), BF16), jax.ShapeDtypeStruct((heads, 1, span), F32)),
        in_specs=[rspec, whole(heads * 64), whole(heads * 64), aspec, aspec, aspec],
        out_specs=(whole(3 * heads * 64), rspec),
        scratch_shapes=[pltpu.VMEM((QB, span), F32), pltpu.VMEM((QB, span), F32), pltpu.VMEM((seq, 128), BF16),
                        pltpu.VMEM((128, seq), BF16), pltpu.VMEM((128, seq), F32)],
        compiler_params=pltpu.CompilerParams(vmem_limit_bytes=56 << 20),
        name="attend_bwd",
    )(rev.reshape(heads, 1, span), dmix, mixed, qa, ka, va)
    return grads, grev.reshape(heads, span)


def on_device(
    inputs,
    teacher,
    lengths,
    buckets,
    gain_attn,
    w_query,
    w_key,
    w_value,
    w_out,
    bias_table,
    gain_ff,
    w_gate,
    w_up,
    w_down,
):
    row_count, model_width = inputs.shape
    group_size = lax.axis_size("tensor")
    seq_len = buckets.shape[0] // 2
    all_rows = row_count * group_size
    local_width = w_query.shape[1]
    heads_here = bias_table.shape[1]
    ff_width = w_gate.shape[1]
    my_first = lax.axis_index("tensor") * row_count
    keep_mine = valid_mask(lengths, my_first, row_count, seq_len)
    keep_all = valid_mask(lengths, 0, all_rows, seq_len)
    reversed_buckets = jnp.concatenate([buckets[:1], jnp.flip(buckets[1:])])
    _, relative = bucket_rows(buckets, bias_table)
    one_hot, backward_relative = bucket_rows(reversed_buckets, bias_table)
    gain_a = gain_attn.astype(jnp.float32)
    gain_f = gain_ff.astype(jnp.float32)
    source = inputs.astype(jnp.float32)
    normed = row_norm(source, gain_a).astype(jnp.bfloat16)
    normed_all = lax.all_gather(normed, "tensor", axis=0, tiled=True)
    w_joint = jnp.concatenate([w_query, w_key, w_value], axis=1)

    joint = jnp.dot(normed_all, w_joint, preferred_element_type=jnp.float32).astype(jnp.bfloat16)
    mixed_parts, query_aug, key_aug, value_aug = attend(lengths, relative, joint, heads_here)
    middle = source + lax.psum_scatter(
        jnp.dot(mixed_parts, w_out, preferred_element_type=jnp.float32).astype(jnp.bfloat16),
        "tensor",
        scatter_dimension=0,
        tiled=True,
    ).astype(jnp.float32)
    normed_ff = row_norm(middle, gain_f).astype(jnp.bfloat16)
    normed_ff_all = lax.all_gather(normed_ff, "tensor", axis=0, tiled=True)
    w_pair = jnp.concatenate([w_gate, w_up], axis=1)
    paired = jnp.dot(normed_ff_all, w_pair, preferred_element_type=jnp.float32)
    gate_values = paired[:, :ff_width]
    up_values = paired[:, ff_width:]
    hidden = geglu_mask(gate_values, up_values, keep_all[:, None]).astype(jnp.bfloat16)
    output = middle + lax.psum_scatter(
        jnp.dot(hidden, w_down, preferred_element_type=jnp.float32).astype(jnp.bfloat16),
        "tensor",
        scatter_dimension=0,
        tiled=True,
    ).astype(jnp.float32)
    activations = output.astype(jnp.bfloat16)
    cotangent = keep_mine[:, None] * (output - teacher.astype(jnp.float32))
    loss_part = jnp.sum(cotangent * cotangent)
    count_part = jnp.sum(keep_mine)
    shard_piece = lax.all_gather(cotangent.astype(jnp.bfloat16), "tensor", axis=0, tiled=True)
    grad_down_acc = lax.dot_general(
        hidden, shard_piece, contract_rows, preferred_element_type=jnp.float32
    )
    grad_rows = lax.dot_general(
        shard_piece, w_down, contract_cols, preferred_element_type=jnp.float32
    )
    grad_down = grad_down_acc
    grad_hidden = grad_rows
    _, geglu_back = jax.vjp(
        lambda gate_in, up_in: geglu_mask(gate_in, up_in, keep_all[:, None]), gate_values, up_values
    )
    grad_gate_rows, grad_up_rows = geglu_back(grad_hidden)
    grad_pair = jnp.concatenate([grad_gate_rows, grad_up_rows], axis=1).astype(jnp.bfloat16)
    grad_w_pair = lax.dot_general(
        normed_ff_all, grad_pair, contract_rows, preferred_element_type=jnp.float32
    )
    grad_normed_ff = lax.psum_scatter(
        lax.dot_general(
            grad_pair, w_pair, contract_cols, preferred_element_type=jnp.float32
        ).astype(jnp.bfloat16),
        "tensor",
        scatter_dimension=0,
        tiled=True,
    ).astype(jnp.float32)
    _, norm_back_ff = jax.vjp(row_norm, middle, gain_f)
    grad_middle_part, grad_gain_ff = norm_back_ff(grad_normed_ff)
    grad_middle = cotangent + grad_middle_part
    shard_piece = lax.all_gather(grad_middle.astype(jnp.bfloat16), "tensor", axis=0, tiled=True)
    grad_out_acc = lax.dot_general(
        mixed_parts, shard_piece, contract_rows, preferred_element_type=jnp.float32
    )
    grad_rows = lax.dot_general(
        shard_piece, w_out, contract_cols, preferred_element_type=jnp.float32
    )
    grad_out = grad_out_acc
    grad_mix = grad_rows.astype(jnp.bfloat16) * keep_all[:, None].astype(jnp.bfloat16)
    grad_parts, grad_relative = attend_back(
        backward_relative, grad_mix, mixed_parts, query_aug, key_aug, value_aug
    )
    grad_w_joint = lax.dot_general(
        normed_all, grad_parts, contract_rows, preferred_element_type=jnp.float32
    )
    grad_table = lax.dot_general(one_hot, grad_relative, contract_table, precision=highest)
    grad_normed = lax.psum_scatter(
        lax.dot_general(
            grad_parts, w_joint, contract_cols, preferred_element_type=jnp.float32
        ).astype(jnp.bfloat16),
        "tensor",
        scatter_dimension=0,
        tiled=True,
    ).astype(jnp.float32)
    _, norm_back_attn = jax.vjp(row_norm, source, gain_a)
    grad_source_part, grad_gain_attn = norm_back_attn(grad_normed)
    grad_source = grad_middle + grad_source_part
    gain_attn_total, gain_ff_total, loss_total, count_total = lax.psum(
        (grad_gain_attn, grad_gain_ff, loss_part, count_part), ("dp", "tensor")
    )
    grad_w_joint, grad_out, grad_table, grad_w_pair, grad_down = lax.psum(
        (grad_w_joint, grad_out, grad_table, grad_w_pair, grad_down), "dp"
    )
    factor = 2.0 / (count_total * model_width)
    loss = loss_total / (count_total * model_width)
    return (
        activations,
        loss,
        grad_source * factor,
        gain_attn_total * factor,
        grad_w_joint[:, :local_width] * factor,
        grad_w_joint[:, local_width : 2 * local_width] * factor,
        grad_w_joint[:, 2 * local_width :] * factor,
        grad_out * factor,
        grad_table * factor,
        gain_ff_total * factor,
        grad_w_pair[:, :ff_width] * factor,
        grad_w_pair[:, ff_width:] * factor,
        grad_down * factor,
    )


def solution(mesh):
    in_specs = (
        P(("dp", "tensor"), None),
        P(("dp", "tensor"), None),
        P("dp"),
        P(),
        P(),
        P(None, "tensor"),
        P(None, "tensor"),
        P(None, "tensor"),
        P("tensor", None),
        P(None, "tensor"),
        P(),
        P(None, "tensor"),
        P(None, "tensor"),
        P("tensor", None),
    )
    out_specs = (
        P(("dp", "tensor"), None),
        P(),
        P(("dp", "tensor"), None),
        P(),
        P(None, "tensor"),
        P(None, "tensor"),
        P(None, "tensor"),
        P("tensor", None),
        P(None, "tensor"),
        P(),
        P(None, "tensor"),
        P(None, "tensor"),
        P("tensor", None),
    )
    return jax.shard_map(
        on_device, mesh=mesh, in_specs=in_specs, out_specs=out_specs, check_vma=False
    )
```

time: 2160 us -> 714 us (0.33)
  local copies, waits for them, and re-layouts: 1340 us -> 16.5 us
  other arithmetic: 252 us -> 33.6 us
  waiting for transfers between devices: 200 us -> 414 us
  matrix products: 269 us -> 58 us
  Pallas kernels: 0 us -> 103 us
    unnamed x163 -> x71, local copies, waits for them, and re-layouts: 586 us -> 8.84 us
    reshape x12 -> x2, local copies, waits for them, and re-layouts: 293 us -> 1.31 us  [the longest x1 0.65 us: attend(): rel.reshape(heads, 1, span)]
    another operation x23 -> x0, local copies, waits for them, and re-layouts: 216 us -> none  [the longest x8 125 us: band_matrix(): tiled = jnp.tile(window, (1, block_rows + 1))]
    dot_general x93 -> x1, matrix products: 218 us -> 4.14 us  [on_device(): jnp.dot(normed_all, w_joint, preferred_element_type=jnp.float32)]
    psum x1, waiting for transfers between devices: 0.01 us -> 191 us  [on_device(): lax.psum((grad_w_joint, grad_out, grad_table, grad_w_pair, grad_down), 'dp')]
    pad x8 -> x0, local copies, waits for them, and re-layouts: 116 us -> none  [the longest x4 67 us: band_matrix(): tiled = tiled[:, block_rows - 1:block_rows - 1 + block_rows * (span - 1)]]
    pallas_call x0 -> x2, Pallas kernels: none -> 103 us  [the longest x1 65 us: attend_back(): pl.pallas_call(bwd_kernel, grid=(heads,), out_shape=(jax.ShapeDtypeStruct...]
    dynamic_update_slice x24 -> x0, other arithmetic: 94.5 us -> none  [the longest x12 88.1 us: one_block(): lax.dynamic_update_slice_in_dim(grad_band, current + grad_scores.astype(j...]
  transfers between devices with their start and end apart: 9 -> 9, of which waited for: 6 -> 8; matrix products, arithmetic and copies ran while one was open for 66% -> 4% of each run, Pallas kernels for 0% -> 0%
where the time goes in v1:
time: 714 us; the launch traced here: 708 us
  waiting for transfers between devices  414 us (58%)
  Pallas kernels  103 us (14%)
  blocking collectives  64.2 us (9%)
  matrix products  58 us (8%)
  other arithmetic  33.6 us (5%)
  between operations  17.7 us (2%)
  local copies, waits for them, and re-layouts  16.5 us (2%)
    psum x1, waiting for transfers between devices, on_device(): lax.psum((grad_w_joint, grad_out, grad_table, grad_w_pair, grad_down), 'dp')  191 us
    pallas_call x1, Pallas kernels, attend_back(): pl.pallas_call(bwd_kernel, grid=(heads,), out_shape=(jax.ShapeDtypeStruct...  65 us
    psum x1, blocking collectives, on_device(): lax.psum((grad_gain_attn, grad_gain_ff, loss_part, count_part), ('dp', 't...  42.9 us
    reduce_scatter x1, waiting for transfers between devices, on_device(): lax.psum_scatter(jnp.dot(hidden, w_down, preferred_element_type=jnp.float...  38 us
    reduce_scatter x1, waiting for transfers between devices, on_device(): lax.psum_scatter(lax.dot_general(grad_pair, w_pair, contract_cols, prefer...  37.8 us
    pallas_call x1, Pallas kernels, attend(): pl.pallas_call(fwd_kernel, grid=(heads,), out_shape=(jax.ShapeDtypeStruct...  37.6 us
    reduce_scatter x1, waiting for transfers between devices, on_device(): lax.psum_scatter(jnp.dot(mixed_parts, w_out, preferred_element_type=jnp.f...  37.5 us
    all_gather x1, waiting for transfers between devices, on_device(): normed_all = lax.all_gather(normed, 'tensor', axis=0, tiled=True)  28.8 us
  transfers between devices with their start and end apart: 9, of which 8 were waited for; matrix products, arithmetic and copies ran while one was open for 4% of the time, Pallas kernels for 0%

profile of v1, /device:TPU:0, one launch (start us, length us, event | category | flops | bytes accessed | tf_op | source)
XLA Modules:
  0.0 707.5 jit_solution(17892103230351095002)
XLA Ops:
  7.3 1.5 fusion.19
  8.8 0.7 convert_element_type.91
  9.5 2.3 fusion.12
  13.5 0.9 copy-done.19
  14.4 28.8 %all-gather.5.cloned.1.call-done = bf16[2048,768]{1,0:T(8,128)(2,1)} async-done(((bf16[512,768]{1,0:T(8,128)(2,1)}), bf16[2048,768]{1,0:T(8,128)(2,1)}) %all-gather.5.cloned.1.call-update) | async-done | bytes 3145744 | tf_op jit(solution)/shard_map/all_gather | solution.py:243
  43.2 4.1 convolution_convert_fusion.4
  47.3 2.6 copy.33.qkv_ref
  49.9 37.6 %attend_fwd.1 = (bf16[2048,192]{1,0:T(8,128)(2,1)}, bf16[3,2048,128]{2,1,0:T(8,128)(2,1)}, bf16[3,2048,128]{2,1,0:T(8,128)(2,1)}, bf16[3,2048,128]{2,1,0:T(8,128)(2,1)}) custom-call(s32[1]{0:T(128)} %copy.47.len_ref, f32[3,1,4096]{2,1,0:T(1,128)} %reshape.151.rel_ref, bf16[2048,576]{1,0:T(8,128)(2,1)} %copy.33.qkv_ref), custom_call_target="tpu_custom_call" | custom-call | tf_op jit(solution)/shard_map/attend_fwd/pallas_call | solution.py:118
  87.5 3.9 convolution_convert_fusion.3
  92.1 37.5 %reduce-scatter.5.cloned.1.call-done = bf16[512,768]{1,0:T(8,128)(2,1)} async-done(((bf16[2048,768]{1,0:T(8,128)(2,1)}), bf16[512,768]{1,0:T(8,128)(2,1)}) %reduce-scatter.5.cloned.1.call-update) | async-done | bytes 786448 | tf_op jit(solution)/shard_map/reduce_scatter | solution.py:248
  129.5 1.5 multiply_reduce_fusion.1
  131.1 1.2 multiply_convert_fusion.2
  132.6 0.9 constant_dynamic-update-slice_fusion.4
  134.0 0.9 constant_dynamic-update-slice_fusion.3
  134.9 26.1 %all-gather.7.cloned.1.call-done = bf16[2048,768]{1,0:T(8,128)(2,1)} async-done(((bf16[512,768]{1,0:T(8,128)(2,1)}), bf16[2048,768]{1,0:T(8,128)(2,1)}) %all-gather.7.cloned.1.call-update) | async-done | bytes 3145744 | tf_op jit(solution)/shard_map/all_gather | solution.py:255
  161.0 6.0 fusion.49
  167.0 1.6 multiply_convert_fusion.1
  168.6 1.7 copy-done.7
  170.3 1.3 copy-done.10
  171.6 3.5 convolution_convert_fusion
  175.2 38.0 %reduce-scatter.7.cloned.1.call-done = bf16[512,768]{1,0:T(8,128)(2,1)} async-done(((bf16[2048,768]{1,0:T(8,128)(2,1)}), bf16[512,768]{1,0:T(8,128)(2,1)}) %reduce-scatter.7.cloned.1.call-update) | async-done | bytes 786448 | tf_op jit(solution)/shard_map/reduce_scatter | solution.py:261
  213.2 2.4 fusion.48
  215.8 28.6 %all-gather.9.cloned.1.call-done = bf16[2048,768]{1,0:T(8,128)(2,1)} async-done(((bf16[512,768]{1,0:T(8,128)(2,1)}), bf16[2048,768]{1,0:T(8,128)(2,1)}) %all-gather.9.cloned.1.call-update) | async-done | bytes 3145744 | tf_op jit(solution)/shard_map/all_gather | solution.py:271
  244.4 7.7 %fusion.6 = (bf16[2048,512]{0,1:T(8,128)(2,1)S(1)}, bf16[2048,512]{0,1:T(8,128)(2,1)S(1)}) fusion(f32[2048,1024]{0,1:T(8,128)} %copy-done.7, f32[2048]{0:T(1024)S(1)} %fusion.35, bf16[2048,768]{1,0:T(8,128)(2,1)} %all-gather.9.cloned.1.call-done, bf16[512,768]{1,0:T(8,128)(2,1)S(1)} %copy-done), kind=kOutput, calls=%fused_computation.10 | convolution fusion | flops 1637875712 | bytes 16523264 | tf_op jit(solution)/shard_map/dot_general | solution.py:275
  252.2 1.3 copy-done.29
  254.2 6.3 convolution_convert_fusion.2
  260.8 37.8 %reduce-scatter.9.cloned.1.call-done = bf16[512,768]{1,0:T(8,128)(2,1)} async-done(((bf16[2048,768]{1,0:T(8,128)(2,1)}), bf16[512,768]{1,0:T(8,128)(2,1)}) %reduce-scatter.9.cloned.1.call-update) | async-done | bytes 786448 | tf_op jit(solution)/shard_map/reduce_scatter | solution.py:288
  298.6 3.0 fusion.14
  301.6 1.7 fusion.47
  305.7 26.3 %all-gather.11.cloned.1.call-done = bf16[2048,768]{1,0:T(8,128)(2,1)} async-done(((bf16[512,768]{1,0:T(8,128)(2,1)}), bf16[2048,768]{1,0:T(8,128)(2,1)}) %all-gather.11.cloned.1.call-update) | async-done | bytes 3145744 | tf_op jit(solution)/shard_map/all_gather | solution.py:299
  332.1 3.9 convolution_convert_fusion.5
  336.0 2.2 copy.34
  338.2 2.5 broadcast_multiply_fusion.1.dmix_ref
  340.7 65.0 %attend_bwd.1 = (bf16[2048,576]{1,0:T(8,128)(2,1)}, f32[3,1,4096]{2,1,0:T(1,128)}) custom-call(f32[3,1,4096]{2,1,0:T(1,128)} %reshape.152.rev_ref, bf16[2048,192]{1,0:T(8,128)(2,1)} %broadcast_multiply_fusion.1.dmix_ref, bf16[2048,192]{1,0:T(8,128)(2,1)} %get-tuple-element.19.mixed_ref, bf16[3,2048,128]{2,1,0:T(8,128)(2,1)} %get-tuple-element.20.qa_ref, ...), custom_call_target="tpu_custom_call" | custom-call | tf_op jit(solution)/shard_map/attend_bwd/pallas_call | solution.py:197
  405.7 6.0 convolution_convert_fusion.1
  412.1 5.6 fusion.52
  417.7 5.1 fusion.7
  422.9 1.6 fusion.51
  425.0 3.4 fusion.50
  429.5 21.4 %psum.68 = f32[32,3]{0,1:T(4,128)S(1)} all-reduce(f32[32,3]{0,1:T(4,128)S(1)} %fusion.22), channel_id=1, replica_groups=mesh['dp'=8,'tensor'=4] {'dp'}, use_global_device_ids=true, to_apply=%region_16.17 | all-reduce | flops 96 | bytes 768 | tf_op jit(solution)/shard_map/psum | solution.py:329
  450.9 1.9 fusion.15
  452.8 42.9 %all-reduce = (f32[]{:T(128)}, f32[]{:T(128)}, f32[768]{0:T(1024)S(1)}, f32[768]{0:T(1024)S(1)}) all-reduce(f32[]{:T(128)} %get-tuple-element.27, f32[]{:T(128)} %fusion.44, f32[768]{0:T(1024)S(1)} %get-tuple-element.28, f32[768]{0:T(1024)S(1)} %get-tuple-element.25), channel_id=1, replica_groups=mesh['dp'=8,'tensor'=4] {'dp','tensor'}, use_global_device_ids=true, to_apply=%region_5.6 | all-reduce | flops 1538 | bytes 12304 | tf_op jit(solution)/shard_map/psum | solution.py:326
  498.3 3.6 fusion.18
  501.9 190.5 %all-reduce.4.cloned.1.call-done = (f32[768,576]{0,1:T(8,128)}, f32[192,768]{1,0:T(8,128)}, f32[768,1024]{1,0:T(8,128)}, f32[512,768]{1,0:T(8,128)}) async-done(((f32[768,576]{0,1:T(8,128)}, f32[192,768]{1,0:T(8,128)}, f32[768,1024]{1,0:T(8,128)}, f32[512,768]{1,0:T(8,128)}), (f32[768,576]{0,1:T(8,128)}, f32[192,768]{1,0:T(8,128)}, f32[768,1024]{1,0:T(8,128)}, ...) | async-done | bytes 7077904 | tf_op jit(solution)/shard_map/psum | solution.py:329
  692.4 2.8 broadcast_multiply_fusion
  695.2 2.1 slice_multiply_fusion
  697.3 0.9 broadcast_multiply_fusion.2
  698.2 1.2 slice_multiply_fusion.2
  (105 shorter events, 9.1 us)
Async XLA Ops:
  7.2 164.4 %copy-start = (bf16[512,768]{1,0:T(8,128)(2,1)S(1)}, bf16[512,768]{1,0:T(8,128)(2,1)}, u32[]{:S(2)}) copy-start(bf16[512,768]{1,0:T(8,128)(2,1)} %param.27) | copy-start | bytes 2359300
  7.2 5.3 copy-start.21
  7.2 5.3 copy-start.28
  7.2 6.1 copy-start.16
  7.2 6.1 copy-start.17
  7.2 35.9 %all-gather.5.cloned.1.call-start = ((), (), s32[]{:S(2)}) async-start(), calls=%async_computation.4 | async-start | bytes 3932160 | tf_op jit(solution)/shard_map/all_gather | solution.py:243
  8.7 4.7 copy-start.18
  11.8 117.8 %reduce-scatter.5.cloned.1.call-start = ((), (), s32[]{:S(2)}) async-start(), calls=%async_computation.5 | async-start | bytes 3932160 | tf_op jit(solution)/shard_map/reduce_scatter | solution.py:248
  13.4 0.9 copy-start.19
  49.9 37.6 %copy-start.15 = (bf16[192,768]{1,0:T(8,128)(2,1)S(1)}, bf16[192,768]{1,0:T(8,128)(2,1)}, u32[]{:S(2)}) copy-start(bf16[192,768]{1,0:T(8,128)(2,1)} %param.22) | copy-start | bytes 884740
  91.4 0.7 copy-start.22
  91.4 38.1 %copy-start.2 = (bf16[512,768]{1,0:T(8,128)(2,1)S(1)}, bf16[512,768]{1,0:T(8,128)(2,1)}, u32[]{:S(2)}) copy-start(bf16[512,768]{1,0:T(8,128)(2,1)} %param.14) | copy-start | bytes 2359300
  91.4 69.6 %all-gather.7.cloned.1.call-start = ((), (), s32[]{:S(2)}) async-start(), calls=%async_computation.6 | async-start | bytes 3932160 | tf_op jit(solution)/shard_map/all_gather | solution.py:255
  92.1 40.5 %copy-start.12 = (bf16[768,512]{1,0:T(8,128)(2,1)S(1)}, bf16[768,512]{1,0:T(8,128)(2,1)}, u32[]{:S(2)}) copy-start(bf16[768,512]{1,0:T(8,128)(2,1)} %param.25) | copy-start | bytes 2359300
  129.5 1.6 copy-start.3
  132.3 80.9 %reduce-scatter.7.cloned.1.call-start = ((), (), s32[]{:S(2)}) async-start(), calls=%async_computation.7 | async-start | bytes 3932160 | tf_op jit(solution)/shard_map/reduce_scatter | solution.py:261
  132.5 1.4 copy-start.13
  167.0 3.3 copy-start.7
  170.3 1.3 copy-start.10
  175.1 38.1 %copy-start.4 = (bf16[512,768]{1,0:T(8,128)(2,1)S(1)}, bf16[512,768]{1,0:T(8,128)(2,1)}, u32[]{:S(2)}) copy-start(bf16[512,768]{1,0:T(8,128)(2,1)} %param.15) | copy-start | bytes 2359300
  175.1 69.3 %all-gather.9.cloned.1.call-start = ((), (), s32[]{:S(2)}) async-start(), calls=%async_computation.8 | async-start | bytes 3932160 | tf_op jit(solution)/shard_map/all_gather | solution.py:271
  215.7 82.9 %reduce-scatter.9.cloned.1.call-start = ((), (), s32[]{:S(2)}) async-start(), calls=%async_computation.9 | async-start | bytes 3932160 | tf_op jit(solution)/shard_map/reduce_scatter | solution.py:288
  252.2 1.4 copy-start.29
  252.2 2.0 copy-start.31
  260.5 38.1 %copy-start.5 = (bf16[512,768]{1,0:T(8,128)(2,1)S(1)}, bf16[512,768]{1,0:T(8,128)(2,1)}, u32[]{:S(2)}) copy-start(bf16[512,768]{1,0:T(8,128)(2,1)} %reduce-scatter.7.cloned.1.call-done) | copy-start | bytes 2359300
  260.5 71.5 %all-gather.11.cloned.1.call-start = ((), (), s32[]{:S(2)}) async-start(), calls=%async_computation.10 | async-start | bytes 3932160 | tf_op jit(solution)/shard_map/all_gather | solution.py:299
  298.6 3.0 copy-start.8
  303.4 147.5 %reduce-scatter.11.cloned.1.call-start = ((), (), s32[]{:S(2)}) async-start(), calls=%async_computation.11 | async-start | bytes 3932160 | tf_op jit(solution)/shard_map/reduce_scatter | solution.py:315
  340.7 65.0 %copy-start.20 = (bf16[768,576]{0,1:T(8,128)(2,1)S(1)}, bf16[768,576]{0,1:T(8,128)(2,1)}, u32[]{:S(2)}) copy-start(bf16[768,576]{0,1:T(8,128)(2,1)} %copy-done.19) | copy-start | bytes 2654212
  411.7 280.7 %all-reduce.4.cloned.1.call-start = ((), (), s32[]{:S(2)}) async-start(), calls=%async_computation.12 | async-start | bytes 14155776 | tf_op jit(solution)/shard_map/psum | solution.py:329
  412.1 5.6 copy-start.24
  412.1 5.6 copy-start.30
  412.1 5.6 copy-start.32
  417.7 5.2 copy-start.6
  417.7 5.2 copy-start.25
  417.7 6.8 copy-start.26
  422.9 2.1 copy-start.23
  428.4 0.8 copy-start.27
  692.4 2.8 copy-start.9
  695.2 2.1 copy-start.14
  695.2 3.0 copy-start.11
  697.3 2.1 copy-start.1
Sparse Core Ops, SparseCore 0:
  11.9 31.2 all-gather.4
  91.5 37.9 reduce-scatter.4
  132.4 28.5 all-gather.6
  175.3 37.9 reduce-scatter.6
  215.8 28.5 all-gather.8
  260.6 37.9 reduce-scatter.8
  303.5 28.5 all-gather.10
  411.9 37.9 reduce-scatter.10
  455.5 236.8 all-reduce.3

commit v2 on v1

--- a/solution.py
+++ b/solution.py
@@ -1,3 +1,5 @@
+import functools
+
 import jax
 import jax.numpy as jnp
 from jax import lax
@@ -6,15 +8,21 @@
 from jax.sharding import PartitionSpec as P
 
 F32, BF16 = jnp.float32, jnp.bfloat16
+MESH = pl.DeviceIdType.MESH
+NT = (((1,), (1,)), ((), ()))
+TN = (((0,), (0,)), ((), ()))
+NN = (((1,), (0,)), ((), ()))
 QB = 256
 KC = 256
-
+CHUNKS = 4
 eps_norm = 1e-06
-masked_score = -1e30
 highest = lax.Precision.HIGHEST
 contract_rows = (((0,), (0,)), ((), ()))
-contract_cols = (((1,), (1,)), ((), ()))
 contract_table = (((0,), (1,)), ((), ()))
+
+
+def dot(a, b, dims=NN):
+    return lax.dot_general(a, b, dims, preferred_element_type=F32)
 
 
 def row_norm(values, gain):
@@ -26,31 +34,11 @@
     return keep_column * jax.nn.gelu(gate_values, approximate=True) * up_values
 
 
-def valid_mask(lengths, first_row, row_count, seq_len):
-    positions = first_row + lax.iota(jnp.int32, row_count)
-    owners = positions // seq_len
-    within = positions % seq_len
-    chosen = owners[:, None] == lax.iota(jnp.int32, lengths.shape[0])[None, :]
-    limits = jnp.sum(jnp.where(chosen, lengths[None, :], 0), axis=1)
-    return (within < limits).astype(jnp.float32)
-
-
 def bucket_rows(buckets, bias_table):
-    one_hot = (buckets[:, None] == lax.iota(jnp.int32, bias_table.shape[0])[None, :]).astype(
-        jnp.float32
-    )
-    relative = lax.dot_general(
-        bias_table.astype(jnp.float32), one_hot, contract_table, precision=highest
-    )
+    one_hot = (buckets[:, None] == lax.iota(jnp.int32, bias_table.shape[0])[None, :]).astype(F32)
+    relative = lax.dot_general(bias_table.astype(F32), one_hot, contract_table, precision=highest)
     return (one_hot, relative)
 
-
-NT = (((1,), (1,)), ((), ()))
-TN = (((0,), (0,)), ((), ()))
-NN = (((1,), (0,)), ((), ()))
-
-def dot(a, b, dims=NN):
-    return lax.dot_general(a, b, dims, preferred_element_type=F32)
 
 def split3(v):
     hi = v.astype(BF16); r = v - hi.astype(F32)
@@ -207,6 +195,296 @@
     return grads, grev.reshape(heads, span)
 
 
+def partners():
+    me = lax.axis_index("tensor")
+    near = me + 1 - 2 * (me % 2)
+    far = (me + 2) % 4
+    return me, near, far, (near + 2) % 4
+
+def meet(*others):
+    barrier = pltpu.get_barrier_semaphore()
+    for other in others:
+        pl.semaphore_signal(barrier, inc=1, device_id=other, device_id_type=MESH)
+    pl.semaphore_wait(barrier, len(others))
+
+def send(src, dst, sems, device):
+    return pltpu.make_async_remote_copy(src_ref=src, dst_ref=dst, send_sem=sems.at[0], recv_sem=sems.at[1],
+                                        device_id=device, device_id_type=MESH)
+
+def gather_kernel(dims, masked, len_ref, x_ref, w_ref, all_ref, y_ref, land, near_sem, far_sem, pass_sem, out_sem):
+    me, near, far, diag = partners()
+    rows = x_ref.shape[0]
+    size = rows // CHUNKS
+    meet({"tensor": near}, {"tensor": far})
+    mine = pl.ds(pl.multiple_of(me * rows, rows), rows)
+    to_near = send(x_ref, land.at[mine], near_sem, {"tensor": near})
+    to_near.start()
+    to_far = []
+    for c in range(CHUNKS):
+        part = pl.ds(pl.multiple_of(me * rows + c * size, size), size)
+        copy = send(x_ref.at[pl.ds(c * size, size)], land.at[part], far_sem.at[c], {"tensor": far})
+        copy.start()
+        to_far.append(copy)
+    own = pltpu.make_async_copy(x_ref, all_ref.at[mine], out_sem.at[0])
+    own.start()
+
+    def project(part, value):
+        y = dot(value, w_ref[...], dims)
+        if masked:
+            pos = part.start + lax.broadcasted_iota(jnp.int32, y.shape, 0)
+            y = jnp.where(pos < len_ref[0], y, 0.0)
+        y_ref[part, :] = y.astype(BF16)
+
+    for c in range(CHUNKS):
+        project(pl.ds(pl.multiple_of(me * rows + c * size, size), size), x_ref[pl.ds(c * size, size), :])
+    to_near.wait_recv()
+    for c in range(CHUNKS):
+        part = pl.ds(pl.multiple_of(near * rows + c * size, size), size)
+        project(part, land[part, :])
+    passed = []
+    for c in range(CHUNKS):
+        to_far[c].wait_recv()
+        part = pl.ds(pl.multiple_of(far * rows + c * size, size), size)
+        copy = send(land.at[part], land.at[part], pass_sem.at[c], {"tensor": near})
+        copy.start()
+        passed.append(copy)
+        project(part, land[part, :])
+    outs = []
+    for i, who in enumerate((near, far)):
+        part = pl.ds(pl.multiple_of(who * rows, rows), rows)
+        copy = pltpu.make_async_copy(land.at[part], all_ref.at[part], out_sem.at[1 + i])
+        copy.start()
+        outs.append(copy)
+    for c in range(CHUNKS):
+        passed[c].wait_recv()
+        part = pl.ds(pl.multiple_of(diag * rows + c * size, size), size)
+        project(part, land[part, :])
+    part = pl.ds(pl.multiple_of(diag * rows, rows), rows)
+    copy = pltpu.make_async_copy(land.at[part], all_ref.at[part], out_sem.at[3])
+    copy.start()
+    outs.append(copy)
+    to_near.wait_send()
+    for copy in to_far + passed:
+        copy.wait_send()
+    own.wait()
+    for copy in outs:
+        copy.wait()
+
+def gather_project(x, w, length, dims, masked, collective_id):
+    rows, width = x.shape
+    out = w.shape[1] if dims is NN else w.shape[0]
+    dma = pltpu.SemaphoreType.DMA
+    vmem = pl.BlockSpec(memory_space=pltpu.VMEM)
+    return pl.pallas_call(
+        functools.partial(gather_kernel, dims, masked),
+        out_shape=(jax.ShapeDtypeStruct((4 * rows, width), BF16), jax.ShapeDtypeStruct((4 * rows, out), BF16)),
+        in_specs=[pl.BlockSpec(memory_space=pltpu.SMEM), vmem, vmem],
+        out_specs=(pl.BlockSpec(memory_space=pl.ANY), vmem),
+        scratch_shapes=[pltpu.VMEM((4 * rows, width), BF16), dma((2,)), dma((CHUNKS, 2)), dma((CHUNKS, 2)), dma((4,))],
+        compiler_params=pltpu.CompilerParams(collective_id=collective_id, has_side_effects=True, vmem_limit_bytes=40 << 20),
+        cost_estimate=pl.CostEstimate(flops=8 * rows * width * out, bytes_accessed=50_000_000, transcendentals=0),
+        name="gather_project",
+    )(length, x, w)
+
+def scatter_kernel(dims, a_ref, w_ref, y_ref, away, kept, out_far, near_land, far_land, near_sem, far_sem):
+    me, near, far, diag = partners()
+    rows = y_ref.shape[0]
+    size = rows // CHUNKS
+    meet({"tensor": near}, {"tensor": far})
+
+    def partial(who, c):
+        return dot(a_ref[pl.ds(pl.multiple_of(who * rows + c * size, size), size), :], w_ref[...], dims)
+
+    copies = []
+    for i, who in enumerate((diag, near)):
+        group = []
+        for c in range(CHUNKS):
+            part = pl.ds(c * size, size)
+            away[i, part, :] = partial(who, c).astype(BF16)
+            copy = send(away.at[i, part], near_land.at[i, part], near_sem.at[i, c], {"tensor": near})
+            copy.start()
+            group.append(copy)
+        copies.append(group)
+        if i == 0:
+            to_far = []
+            for c in range(CHUNKS):
+                part = pl.ds(c * size, size)
+                mine = partial(far, c)
+                group[c].wait_recv()
+                out_far[part, :] = (mine + near_land[0, part, :].astype(F32)).astype(BF16)
+                copy = send(out_far.at[part], far_land.at[part], far_sem.at[c], {"tensor": far})
+                copy.start()
+                to_far.append(copy)
+    for c in range(CHUNKS):
+        part = pl.ds(c * size, size)
+        mine = partial(me, c)
+        copies[1][c].wait_recv()
+        kept[part, :] = mine + near_land[1, part, :].astype(F32)
+    for c in range(CHUNKS):
+        part = pl.ds(c * size, size)
+        to_far[c].wait_recv()
+        y_ref[part, :] = kept[part, :] + far_land[part, :].astype(F32)
+    for copy in copies[0] + copies[1] + to_far:
+        copy.wait_send()
+
+def project_scatter(a, w, dims, collective_id):
+    rows = a.shape[0] // 4
+    out = w.shape[1] if dims is NN else w.shape[0]
+    dma = pltpu.SemaphoreType.DMA
+    vmem = pl.BlockSpec(memory_space=pltpu.VMEM)
+    return pl.pallas_call(
+        functools.partial(scatter_kernel, dims),
+        out_shape=jax.ShapeDtypeStruct((rows, out), F32),
+        in_specs=[vmem, vmem],
+        out_specs=vmem,
+        scratch_shapes=[pltpu.VMEM((2, rows, out), BF16), pltpu.VMEM((rows, out), F32), pltpu.VMEM((rows, out), BF16),
+                        pltpu.VMEM((2, rows, out), BF16), pltpu.VMEM((rows, out), BF16), dma((2, CHUNKS, 2)), dma((CHUNKS, 2))],
+        compiler_params=pltpu.CompilerParams(collective_id=collective_id, has_side_effects=True, vmem_limit_bytes=40 << 20),
+        cost_estimate=pl.CostEstimate(flops=8 * rows * a.shape[1] * out, bytes_accessed=50_000_000, transcendentals=0),
+        name="project_scatter",
+    )(a, w)
+
+
+def reduce_kernel(count, pads, *refs):
+    n = lax.axis_size("dp")
+    outer = n // 2
+    gs, small = refs[:count], refs[count]
+    outs, small_out = refs[count + 1:2 * count + 1], refs[2 * count + 1]
+    rest = refs[2 * count + 2:]
+    works, lands, sums, zlands = (rest[i * count:(i + 1) * count] for i in range(4))
+    sland, szland, xsem, zsem, gsem, bsem, ssem, szsem = rest[4 * count:]
+    d = lax.axis_index("dp")
+    side, o = d % 2, d // 2
+    pair = {"dp": d + 1 - 2 * side}
+    me, near, far, _ = partners()
+    others = [{"dp": ((o + j) % outer) * 2 + side} for j in range(1, outer)]
+    meet(pair, *others, {"tensor": near}, {"tensor": far})
+
+    def rows(k, which, piece=None):
+        half = pads[k] // 2
+        if piece is None:
+            return pl.ds(pl.multiple_of(which * half, 16), half)
+        size = half // outer
+        return pl.ds(pl.multiple_of(which * half + piece * size, 16), size)
+
+    started = []
+
+    def go(copy):
+        copy.start()
+        started.append(copy)
+        return copy
+
+    pending = {}
+
+    def stage0(k):
+        g = gs[k]
+        if pads[k] == g.shape[0]:
+            src = g
+        else:
+            works[k][0:g.shape[0], :] = g[...]
+            src = works[k]
+        pending[k, 0] = [go(send(src.at[rows(k, 1 - side)], lands[k], xsem.at[k], pair))]
+        return src
+
+    srcs = {}
+
+    def stage1(k):
+        pending[k, 0][0].wait_recv()
+        half = pads[k] // 2
+        sums[k][...] = (srcs[k][rows(k, side), :].astype(F32) + lands[k][...].astype(F32)).astype(BF16)
+        size = half // outer
+        pending[k, 1] = []
+        for j in range(1, outer):
+            piece = pl.ds(pl.multiple_of(((o + j) % outer) * size, 16), size)
+            pending[k, 1].append(go(send(sums[k].at[piece], zlands[k].at[j - 1], zsem.at[k, j - 1], others[j - 1])))
+
+    def stage2(k):
+        half = pads[k] // 2
+        size = half // outer
+        total = sums[k][pl.ds(pl.multiple_of(o * size, 16), size), :].astype(F32)
+        for j in range(1, outer):
+            pending[k, 1][j - 1].wait_recv()
+            total = total + zlands[k][j - 1].astype(F32)
+        mine = rows(k, side, o)
+        works[k][mine, :] = total.astype(BF16)
+        pending[k, 2] = [go(send(works[k].at[mine], works[k].at[mine], gsem.at[k, j - 1], others[j - 1])) for j in range(1, outer)]
+
+    def stage3(k):
+        for copy in pending[k, 2]:
+            copy.wait_recv()
+        mine = rows(k, side)
+        pending[k, 3] = [go(send(works[k].at[mine], works[k].at[mine], bsem.at[k], pair))]
+
+    def stage4(k):
+        pending[k, 3][0].wait_recv()
+        outs[k][...] = works[k][0:outs[k].shape[0], :]
+
+    stages = (stage0, stage1, stage2, stage3, stage4)
+
+    def small0():
+        sland[0] = small[...]
+        pending["s", 0] = go(send(sland.at[0], sland.at[1], ssem.at[0], pair))
+
+    def small1():
+        pending["s", 0].wait_recv()
+        szland[o] = sland[0] + sland[1]
+        pending["s", 1] = [go(send(szland.at[o], szland.at[o], szsem.at[j - 1], others[j - 1])) for j in range(1, outer)]
+
+    def small2():
+        for copy in pending["s", 1]:
+            copy.wait_recv()
+        total = szland[0]
+        for j in range(1, outer):
+            total = total + szland[j]
+        sland[2] = total
+        pending["s", 2] = go(send(sland.at[2], sland.at[3], ssem.at[1], {"tensor": near}))
+
+    def small3():
+        pending["s", 2].wait_recv()
+        sland[4] = sland[2] + sland[3]
+        pending["s", 3] = go(send(sland.at[4], sland.at[5], ssem.at[2], {"tensor": far}))
+
+    def small4():
+        pending["s", 3].wait_recv()
+        own = lax.broadcasted_iota(jnp.int32, small.shape, 0) >= small.shape[0] - 1
+        small_out[...] = jnp.where(own, sland[2], sland[4] + sland[5])
+
+    smalls = (small0, small1, small2, small3, small4)
+    for step in range(count + 4):
+        if step < 5:
+            smalls[step]()
+        for k in range(count):
+            at = step - k
+            if 0 <= at < 5:
+                made = stages[at](k)
+                if at == 0:
+                    srcs[k] = made
+    for copy in started:
+        copy.wait_send()
+
+def reduce_all(arrays, small, n, collective_id):
+    outer = n // 2
+    count = len(arrays)
+    pads = [-(-a.shape[0] // (16 * n)) * 16 * n for a in arrays]
+    dma = pltpu.SemaphoreType.DMA
+    vmem = pl.BlockSpec(memory_space=pltpu.VMEM)
+    halves = [p // 2 for p in pads]
+    return pl.pallas_call(
+        functools.partial(reduce_kernel, count, pads),
+        out_shape=tuple(jax.ShapeDtypeStruct(a.shape, BF16) for a in arrays) + (jax.ShapeDtypeStruct(small.shape, F32),),
+        in_specs=[vmem] * (count + 1),
+        out_specs=(vmem,) * (count + 1),
+        scratch_shapes=[pltpu.VMEM((p, a.shape[1]), BF16) for p, a in zip(pads, arrays)]
+        + [pltpu.VMEM((h, a.shape[1]), BF16) for h, a in zip(halves, arrays)]
+        + [pltpu.VMEM((h, a.shape[1]), BF16) for h, a in zip(halves, arrays)]
+        + [pltpu.VMEM((outer - 1, h // outer, a.shape[1]), BF16) for h, a in zip(halves, arrays)]
+        + [pltpu.VMEM((6,) + small.shape, F32), pltpu.VMEM((outer,) + small.shape, F32),
+           dma((count, 2)), dma((count, outer - 1, 2)), dma((count, outer - 1, 2)), dma((count, 2)), dma((3, 2)), dma((outer - 1, 2))],
+        compiler_params=pltpu.CompilerParams(collective_id=collective_id, has_side_effects=True, vmem_limit_bytes=50 << 20),
+        name="reduce_all",
+    )(*arrays, small)
+
+
 def on_device(
     inputs,
     teacher,
@@ -225,126 +503,114 @@
 ):
     row_count, model_width = inputs.shape
     group_size = lax.axis_size("tensor")
+    dp_size = lax.axis_size("dp")
     seq_len = buckets.shape[0] // 2
-    all_rows = row_count * group_size
     local_width = w_query.shape[1]
     heads_here = bias_table.shape[1]
     ff_width = w_gate.shape[1]
     my_first = lax.axis_index("tensor") * row_count
-    keep_mine = valid_mask(lengths, my_first, row_count, seq_len)
-    keep_all = valid_mask(lengths, 0, all_rows, seq_len)
+    keep_mine = (my_first + lax.iota(jnp.int32, row_count) < lengths[0]).astype(F32)[:, None]
     reversed_buckets = jnp.concatenate([buckets[:1], jnp.flip(buckets[1:])])
     _, relative = bucket_rows(buckets, bias_table)
     one_hot, backward_relative = bucket_rows(reversed_buckets, bias_table)
-    gain_a = gain_attn.astype(jnp.float32)
-    gain_f = gain_ff.astype(jnp.float32)
-    source = inputs.astype(jnp.float32)
-    normed = row_norm(source, gain_a).astype(jnp.bfloat16)
-    normed_all = lax.all_gather(normed, "tensor", axis=0, tiled=True)
+    gain_a = gain_attn.astype(F32)
+    gain_f = gain_ff.astype(F32)
+    source = inputs.astype(F32)
+    normed = row_norm(source, gain_a).astype(BF16)
     w_joint = jnp.concatenate([w_query, w_key, w_value], axis=1)
-
-    joint = jnp.dot(normed_all, w_joint, preferred_element_type=jnp.float32).astype(jnp.bfloat16)
+    normed_all, joint = gather_project(normed, w_joint, lengths, NN, False, 1)
+
+    near_pairs = [(i, i ^ 1) for i in range(group_size)]
+    far_pairs = [(i, i ^ 2) for i in range(group_size)]
+    near_of = lambda value: lax.ppermute(value, "tensor", near_pairs)
+    far_of = lambda value: lax.ppermute(value, "tensor", far_pairs)
+    w_pair = jnp.concatenate([w_gate, w_up], axis=1)
+    pairs = [w_pair, near_of(w_pair), far_of(w_pair)]
+    downs = [w_down, near_of(w_down), far_of(w_down)]
+    pairs.append(near_of(pairs[2]))
+    downs.append(near_of(downs[2]))
+
     mixed_parts, query_aug, key_aug, value_aug = attend(lengths, relative, joint, heads_here)
-    middle = source + lax.psum_scatter(
-        jnp.dot(mixed_parts, w_out, preferred_element_type=jnp.float32).astype(jnp.bfloat16),
-        "tensor",
-        scatter_dimension=0,
-        tiled=True,
-    ).astype(jnp.float32)
-    normed_ff = row_norm(middle, gain_f).astype(jnp.bfloat16)
-    normed_ff_all = lax.all_gather(normed_ff, "tensor", axis=0, tiled=True)
-    w_pair = jnp.concatenate([w_gate, w_up], axis=1)
-    paired = jnp.dot(normed_ff_all, w_pair, preferred_element_type=jnp.float32)
-    gate_values = paired[:, :ff_width]
-    up_values = paired[:, ff_width:]
-    hidden = geglu_mask(gate_values, up_values, keep_all[:, None]).astype(jnp.bfloat16)
-    output = middle + lax.psum_scatter(
-        jnp.dot(hidden, w_down, preferred_element_type=jnp.float32).astype(jnp.bfloat16),
-        "tensor",
-        scatter_dimension=0,
-        tiled=True,
-    ).astype(jnp.float32)
-    activations = output.astype(jnp.bfloat16)
-    cotangent = keep_mine[:, None] * (output - teacher.astype(jnp.float32))
+    middle = source + project_scatter(mixed_parts, w_out, NN, 2)
+    normed_ff = row_norm(middle, gain_f).astype(BF16)
+    gates, ups, hiddens = [], [], []
+    output = middle
+    for pair, down in zip(pairs, downs):
+        paired = dot(normed_ff, pair)
+        gates.append(paired[:, :ff_width])
+        ups.append(paired[:, ff_width:])
+        hiddens.append(geglu_mask(gates[-1], ups[-1], keep_mine).astype(BF16))
+        output = output + dot(hiddens[-1], down)
+    activations = output.astype(BF16)
+    cotangent = keep_mine * (output - teacher.astype(F32))
     loss_part = jnp.sum(cotangent * cotangent)
     count_part = jnp.sum(keep_mine)
-    shard_piece = lax.all_gather(cotangent.astype(jnp.bfloat16), "tensor", axis=0, tiled=True)
-    grad_down_acc = lax.dot_general(
-        hidden, shard_piece, contract_rows, preferred_element_type=jnp.float32
-    )
-    grad_rows = lax.dot_general(
-        shard_piece, w_down, contract_cols, preferred_element_type=jnp.float32
-    )
-    grad_down = grad_down_acc
-    grad_hidden = grad_rows
-    _, geglu_back = jax.vjp(
-        lambda gate_in, up_in: geglu_mask(gate_in, up_in, keep_all[:, None]), gate_values, up_values
-    )
-    grad_gate_rows, grad_up_rows = geglu_back(grad_hidden)
-    grad_pair = jnp.concatenate([grad_gate_rows, grad_up_rows], axis=1).astype(jnp.bfloat16)
-    grad_w_pair = lax.dot_general(
-        normed_ff_all, grad_pair, contract_rows, preferred_element_type=jnp.float32
-    )
-    grad_normed_ff = lax.psum_scatter(
-        lax.dot_general(
-            grad_pair, w_pair, contract_cols, preferred_element_type=jnp.float32
-        ).astype(jnp.bfloat16),
-        "tensor",
-        scatter_dimension=0,
-        tiled=True,
-    ).astype(jnp.float32)
+    grad_ff_rows = cotangent.astype(BF16)
+    grad_normed_ff = 0.0
+    down_grads, pair_grads = [], []
+    for pair, down, gate, up, hidden in zip(pairs, downs, gates, ups, hiddens):
+        grad_hidden = dot(grad_ff_rows, down, NT)
+        _, geglu_back = jax.vjp(lambda g, u: geglu_mask(g, u, keep_mine), gate, up)
+        grad_pair = jnp.concatenate(geglu_back(grad_hidden), axis=1).astype(BF16)
+        grad_normed_ff = grad_normed_ff + dot(grad_pair, pair, NT)
+        down_grads.append(dot(hidden, grad_ff_rows, TN))
+        pair_grads.append(dot(normed_ff, grad_pair, TN))
     _, norm_back_ff = jax.vjp(row_norm, middle, gain_f)
     grad_middle_part, grad_gain_ff = norm_back_ff(grad_normed_ff)
     grad_middle = cotangent + grad_middle_part
-    shard_piece = lax.all_gather(grad_middle.astype(jnp.bfloat16), "tensor", axis=0, tiled=True)
-    grad_out_acc = lax.dot_general(
-        mixed_parts, shard_piece, contract_rows, preferred_element_type=jnp.float32
-    )
-    grad_rows = lax.dot_general(
-        shard_piece, w_out, contract_cols, preferred_element_type=jnp.float32
-    )
-    grad_out = grad_out_acc
-    grad_mix = grad_rows.astype(jnp.bfloat16) * keep_all[:, None].astype(jnp.bfloat16)
+
+    def share(parts):
+        mine, near, far, diag = parts
+        total_far = (far + near_of(diag.astype(BF16)).astype(F32)).astype(BF16)
+        return (mine + near_of(near.astype(BF16)).astype(F32) + far_of(total_far).astype(F32)).astype(BF16)
+
+    grad_down = share(down_grads)
+    grad_pair_sum = share(pair_grads)
+    grad_all, grad_mix = gather_project(grad_middle.astype(BF16), w_out, lengths, NT, True, 3)
+    grad_out = dot(mixed_parts, grad_all, TN).astype(BF16)
     grad_parts, grad_relative = attend_back(
         backward_relative, grad_mix, mixed_parts, query_aug, key_aug, value_aug
     )
-    grad_w_joint = lax.dot_general(
-        normed_all, grad_parts, contract_rows, preferred_element_type=jnp.float32
-    )
+    grad_w_joint = dot(normed_all, grad_parts, TN).astype(BF16)
     grad_table = lax.dot_general(one_hot, grad_relative, contract_table, precision=highest)
-    grad_normed = lax.psum_scatter(
-        lax.dot_general(
-            grad_parts, w_joint, contract_cols, preferred_element_type=jnp.float32
-        ).astype(jnp.bfloat16),
-        "tensor",
-        scatter_dimension=0,
-        tiled=True,
-    ).astype(jnp.float32)
+    grad_normed = project_scatter(grad_parts, w_joint, NT, 4)
     _, norm_back_attn = jax.vjp(row_norm, source, gain_a)
     grad_source_part, grad_gain_attn = norm_back_attn(grad_normed)
     grad_source = grad_middle + grad_source_part
-    gain_attn_total, gain_ff_total, loss_total, count_total = lax.psum(
-        (grad_gain_attn, grad_gain_ff, loss_part, count_part), ("dp", "tensor")
+
+    gain_rows = model_width // 128
+    scalars = jnp.zeros((8, 128), F32).at[0, 0].set(loss_part).at[0, 1].set(count_part)
+    table_row = jnp.zeros((8, 128), F32).at[7, : grad_table.size].set(grad_table.reshape(-1))
+    small = jnp.concatenate(
+        [grad_gain_attn.reshape(gain_rows, 128), grad_gain_ff.reshape(gain_rows, 128), scalars, table_row]
     )
-    grad_w_joint, grad_out, grad_table, grad_w_pair, grad_down = lax.psum(
-        (grad_w_joint, grad_out, grad_table, grad_w_pair, grad_down), "dp"
+    small = jnp.pad(small, ((small.shape[0] % 8, 0), (0, 0)))
+    first = small.shape[0] - 16 - 2 * gain_rows
+    rows_here = grad_out.shape[0]
+    tall = jnp.concatenate([grad_out, grad_down])
+    tall = jnp.pad(tall, ((0, -tall.shape[0] % (16 * dp_size)), (0, 0)))
+    grad_gate, grad_up, tall, grad_w_joint, small = reduce_all(
+        [grad_pair_sum[:, :ff_width], grad_pair_sum[:, ff_width:], tall, grad_w_joint], small, dp_size, 5
     )
+    small = small[first:]
+    loss_total, count_total = small[2 * gain_rows, 0], small[2 * gain_rows, 1]
+    grad_table = small[-1, : grad_table.size].reshape(grad_table.shape)
     factor = 2.0 / (count_total * model_width)
-    loss = loss_total / (count_total * model_width)
+    scaled = lambda value: value.astype(F32) * factor
     return (
         activations,
-        loss,
+        loss_total / (count_total * model_width),
         grad_source * factor,
-        gain_attn_total * factor,
-        grad_w_joint[:, :local_width] * factor,
-        grad_w_joint[:, local_width : 2 * local_width] * factor,
-        grad_w_joint[:, 2 * local_width :] * factor,
-        grad_out * factor,
+        small[:gain_rows].reshape(-1) * factor,
+        scaled(grad_w_joint[:, :local_width]),
+        scaled(grad_w_joint[:, local_width : 2 * local_width]),
+        scaled(grad_w_joint[:, 2 * local_width :]),
+        scaled(tall[:rows_here]),
         grad_table * factor,
-        gain_ff_total * factor,
-        grad_w_pair[:, :ff_width] * factor,
-        grad_w_pair[:, ff_width:] * factor,
-        grad_down * factor,
+        small[gain_rows : 2 * gain_rows].reshape(-1) * factor,
+        scaled(grad_gate),
+        scaled(grad_up),
+        scaled(tall[rows_here : rows_here + ff_width]),
     )
 
 

time: 714 us -> 514 us (0.72)
  waiting for transfers between devices: 414 us -> 45.6 us
  Pallas kernels: 103 us -> 339 us
  blocking collectives: 64.2 us -> 0 us
  local copies, waits for them, and re-layouts: 16.5 us -> 30.1 us
  between operations: 17.7 us -> 5.03 us
  other arithmetic: 33.6 us -> 24.3 us
    pallas_call x0 -> x5, Pallas kernels: none -> 234 us  [the longest x1 103 us: reduce_all(): pl.pallas_call(functools.partial(reduce_kernel, count, pads), out_shape=t...]
    psum x1 -> x0, waiting for transfers between devices: 191 us -> none  [on_device(): lax.psum((grad_w_joint, grad_out, grad_table, grad_w_pair, grad_down), 'dp')]
    reduce_scatter x4 -> x0, waiting for transfers between devices: 113 us -> none  [the longest x1 38 us: on_device(): lax.psum_scatter(jnp.dot(hidden, w_down, preferred_element_type=jnp.float...]
    all_gather x4 -> x0, waiting for transfers between devices: 110 us -> none  [the longest x1 28.8 us: on_device(): normed_all = lax.all_gather(normed, 'tensor', axis=0, tiled=True)]
    psum x2 -> x0, blocking collectives: 64.2 us -> none  [the longest x1 42.9 us: on_device(): lax.psum((grad_gain_attn, grad_gain_ff, loss_part, count_part), ('dp', 't...]
    ppermute x0 -> x12, waiting for transfers between devices: none -> 45.6 us  [the longest x4 45.5 us: on_device(): far_of = lambda value: lax.ppermute(value, 'tensor', far_pairs)]
    unnamed x71 -> x84, local copies, waits for them, and re-layouts: 8.84 us -> 20.6 us
    dot_general x14 -> x28, matrix products: 57.6 us -> 52.4 us  [the longest x26 52 us: dot(): return lax.dot_general(a, b, dims, preferred_element_type=F32)]
  transfers between devices with their start and end apart: 9 -> 12, of which waited for: 8 -> 1; matrix products, arithmetic and copies ran while one was open for 4% -> 14% of each run, Pallas kernels for 0% -> 47%
where the time goes in v2:
time: 514 us; the launch traced here: 504 us
  Pallas kernels  339 us (66%)
  matrix products  52.7 us (10%)
  waiting for transfers between devices  45.6 us (9%)
  local copies, waits for them, and re-layouts  30.1 us (6%)
  other arithmetic  24.3 us (5%)
  starting transfers between devices  7.11 us (1%)
    pallas_call x1, Pallas kernels, reduce_all(): pl.pallas_call(functools.partial(reduce_kernel, count, pads), out_shape=t...  103 us
    pallas_call x2, Pallas kernels, gather_project(): pl.pallas_call(functools.partial(gather_kernel, dims, masked), out_shape=...  85.9 us
    pallas_call x1, Pallas kernels, attend_back(): pl.pallas_call(bwd_kernel, grid=(heads,), out_shape=(jax.ShapeDtypeStruct...  66.2 us
    dot_general x26, matrix products, dot(): return lax.dot_general(a, b, dims, preferred_element_type=F32)  52 us
    ppermute x4, waiting for transfers between devices, on_device(): far_of = lambda value: lax.ppermute(value, 'tensor', far_pairs)  45.5 us
    pallas_call x2, Pallas kernels, project_scatter(): pl.pallas_call(functools.partial(scatter_kernel, dims), out_shape=jax.Sha...  44.4 us
    pallas_call x1, Pallas kernels, attend(): pl.pallas_call(fwd_kernel, grid=(heads,), out_shape=(jax.ShapeDtypeStruct...  39 us
    unnamed x84, local copies, waits for them, and re-layouts  20.6 us
  transfers between devices with their start and end apart: 12, of which 1 were waited for; matrix products, arithmetic and copies ran while one was open for 14% of the time, Pallas kernels for 47%

profile of v2, /device:TPU:0, one launch (start us, length us, event | category | flops | bytes accessed | tf_op | source)
XLA Modules:
  0.0 503.6 jit_solution(2226496186976906490)
XLA Ops:
  1.2 2.6 collective-permute-start.3
  3.8 2.1 constant_dynamic-update-slice_fusion.1
  10.7 64.2 %gather_project.2 = (bf16[2048,768]{1,0:T(8,128)(2,1)S(1)}, bf16[2048,576]{1,0:T(8,128)(2,1)S(1)}) custom-call(s32[1]{0:T(128)} %copy.124.len_ref, bf16[512,768]{1,0:T(8,128)(2,1)S(1)} %fusion.4.x_ref, bf16[768,576]{1,0:T(8,128)(2,1)S(1)} %pad_maximum_fusion.4.w_ref), custom_call_target="tpu_custom_call" | custom-call | flops 1811939328 | bytes 50000000 | tf_op jit(solution)/shard_map/gather_project/pallas_call | solution.py:278
  74.9 1.5 copy-done.4
  76.4 1.6 copy-done.10
  78.0 39.0 %attend_fwd.1 = (bf16[2048,192]{1,0:T(8,128)(2,1)}, bf16[3,2048,128]{2,1,0:T(8,128)(2,1)}, bf16[3,2048,128]{2,1,0:T(8,128)(2,1)}, bf16[3,2048,128]{2,1,0:T(8,128)(2,1)}) custom-call(s32[1]{0:T(128)} %copy.124.len_ref, f32[3,1,4096]{2,1,0:T(1,128)} %reshape.199.rel_ref, bf16[2048,576]{1,0:T(8,128)(2,1)} %copy-done.4), custom_call_target="tpu_custom_call" | custom-call | tf_op jit(solution)/shard_map/attend_fwd/pallas_call | solution.py:106
  118.2 21.9 %project_scatter.2 = f32[512,768]{1,0:T(8,128)S(1)} custom-call(bf16[2048,192]{1,0:T(8,128)(2,1)S(1)} %copy-done.2, bf16[192,768]{1,0:T(8,128)(2,1)S(1)} %copy-done.6), custom_call_target="tpu_custom_call" | custom-call | flops 603979776 | bytes 50000000 | tf_op jit(solution)/shard_map/project_scatter/pallas_call | solution.py:335
  143.6 2.7 fusion.69
  146.7 2.4 fusion.73
  149.1 2.4 fusion.71
  151.5 2.4 fusion.75
  153.9 1.8 multiply_convert_fusion.5
  156.3 1.7 fusion.74
  158.1 1.8 fusion.72
  160.8 1.5 convolution_convert_fusion.3
  162.3 1.5 convolution_convert_fusion.4
  165.0 1.7 fusion.78
  166.7 1.7 fusion.77
  168.5 4.9 fusion.25
  173.4 3.1 fusion.43
  176.6 2.2 convolution_convert_fusion
  178.8 2.2 convolution_convert_fusion.1
  180.9 2.4 fusion.42
  183.4 2.4 fusion.40
  185.8 3.0 multiply_reduce_fusion.1
  189.3 2.9 fusion.64
  192.2 21.7 %gather_project.3 = (bf16[2048,768]{1,0:T(8,128)(2,1)S(1)}, bf16[2048,192]{1,0:T(8,128)(2,1)S(1)}) custom-call(s32[1]{0:T(128)} %copy.124.len_ref, bf16[512,768]{1,0:T(8,128)(2,1)S(1)} %get-tuple-element.148.x_ref, bf16[192,768]{1,0:T(8,128)(2,1)S(1)} %copy-done.6), custom_call_target="tpu_custom_call" | custom-call | flops 603979776 | bytes 50000000 | tf_op jit(solution)/shard_map/gather_project/pallas_call | solution.py:278
  214.9 1.7 copy-done.8
  216.6 66.2 %attend_bwd.1 = (bf16[2048,576]{1,0:T(8,128)(2,1)}, f32[3,1,4096]{2,1,0:T(1,128)}) custom-call(f32[3,1,4096]{2,1,0:T(1,128)} %reshape.200.rev_ref, bf16[2048,192]{1,0:T(8,128)(2,1)} %copy-done.5, bf16[2048,192]{1,0:T(8,128)(2,1)} %get-tuple-element.65.a_ref.mixed_ref, bf16[3,2048,128]{2,1,0:T(8,128)(2,1)} %get-tuple-element.69.qa_ref, ...), custom_call_target="tpu_custom_call" | custom-call | tf_op jit(solution)/shard_map/attend_bwd/pallas_call | solution.py:185
  282.8 1.7 copy-done.7
  284.5 22.5 %project_scatter.3 = f32[512,768]{1,0:T(8,128)S(1)} custom-call(bf16[2048,576]{1,0:T(8,128)(2,1)S(1)} %copy-done.7, bf16[768,576]{1,0:T(8,128)(2,1)S(1)} %pad_maximum_fusion.4.w_ref), custom_call_target="tpu_custom_call" | custom-call | flops 1811939328 | bytes 50000000 | tf_op jit(solution)/shard_map/project_scatter/pallas_call | solution.py:335
  307.7 3.1 convolution_convert_fusion.2
  311.2 2.2 copy.107.refs_3_
  314.1 2.3 scatter.11
  317.6 2.7 add_convert_fusion.1
  320.4 1.4 collective-permute-start.8
  321.8 1.7 add_convert_fusion.3
  327.3 45.5 %collective-permute-done.11 = bf16[512,768]{1,0:T(8,128)(2,1)S(1)} collective-permute-done((bf16[512,768]{1,0:T(8,128)(2,1)S(1)}, bf16[512,768]{1,0:T(8,128)(2,1)S(1)}, u32[]{:S(2)}, u32[]{:S(2)}) %collective-permute-start.11) | collective-permute-done | bytes 786464 | tf_op jit(solution)/shard_map/ppermute | solution.py:526
  372.9 1.4 add_convert_fusion.2
  375.4 2.3 add_convert_fusion
  377.9 103.3 %reduce_all.1 = (bf16[768,512]{1,0:T(8,128)(2,1)S(1)}, bf16[768,512]{1,0:T(8,128)(2,1)S(1)}, bf16[768,768]{1,0:T(8,128)(2,1)}, bf16[768,576]{1,0:T(8,128)(2,1)}, f32[32,128]{1,0:T(8,128)S(1)}) custom-call(bf16[768,512]{1,0:T(8,128)(2,1)S(1)} %get-tuple-element.163.refs_0_, bf16[768,512]{1,0:T(8,128)(2,1)S(1)} %get-tuple-element.162.refs_1_, ...), custom_call_target="tpu_custom_call" | custom-call | tf_op jit(solution)/shard_map/reduce_all/pallas_call | solution.py:472
  483.7 1.8 convert_multiply_fusion.10
  486.3 2.9 convert_multiply_fusion.7
  489.2 2.2 copy.110
  491.4 2.2 copy.109
  493.6 2.2 copy.108
  495.8 4.1 fusion.8
  499.9 2.1 convert_multiply_fusion.5
  (138 shorter events, 23.7 us)
Async XLA Ops:
  0.6 6.9 %copy-start = (bf16[32,3]{0,1:T(4,128)(2,1)S(1)}, bf16[32,3]{0,1:T(4,128)(2,1)}, u32[]{:S(2)}) copy-start(bf16[32,3]{0,1:T(4,128)(2,1)} %param.29) | copy-start | bytes 580
  0.7 5.2 %copy-start.23 = (bf16[768,512]{1,0:T(8,128)(2,1)S(1)}, bf16[768,512]{1,0:T(8,128)(2,1)}, u32[]{:S(2)}) copy-start(bf16[768,512]{1,0:T(8,128)(2,1)} %param.32) | copy-start | bytes 2359300
  0.7 6.3 %copy-start.28 = (bf16[768,192]{0,1:T(8,128)(2,1)S(1)}, bf16[768,192]{0,1:T(8,128)(2,1)}, u32[]{:S(2)}) copy-start(bf16[768,192]{0,1:T(8,128)(2,1)} %param.25) | copy-start | bytes 884740
  0.7 6.5 %copy-start.29 = (bf16[768,192]{0,1:T(8,128)(2,1)S(1)}, bf16[768,192]{0,1:T(8,128)(2,1)}, u32[]{:S(2)}) copy-start(bf16[768,192]{0,1:T(8,128)(2,1)} %param.26) | copy-start | bytes 884740
  0.7 157.4 %collective-permute-start.1 = (bf16[512,768]{1,0:T(8,128)(2,1)}, bf16[512,768]{1,0:T(8,128)(2,1)}, u32[]{:S(2)}, u32[]{:S(2)}) collective-permute-start(bf16[512,768]{1,0:T(8,128)(2,1)} %param.33), channel_id=1, source_target_pairs={{0,1},{1,0},{2,3},{3,2},{4,5},{5,4},{6,7},{7,6},{8,9},{9,8},{10,11... | collective-permute-start | bytes 2359304 | tf_op jit(solution)/shard_map/ppermute | solution.py:525
  1.2 145.0 %collective-permute-start.3 = (bf16[512,768]{1,0:T(8,128)(2,1)}, bf16[512,768]{1,0:T(8,128)(2,1)}, u32[]{:S(2)}, u32[]{:S(2)}) collective-permute-start(bf16[512,768]{1,0:T(8,128)(2,1)} %param.33), channel_id=1, source_target_pairs={{0,2},{1,3},{2,0},{3,1},{4,6},{5,7},{6,4},{7,5},{8,10},{9,11},{10,... | collective-permute-start | bytes 2359304 | tf_op jit(solution)/shard_map/ppermute | solution.py:526
  5.9 1.5 copy-start.30
  5.9 1.7 copy-start.31
  6.8 134.5 %collective-permute-start.2 = (bf16[768,1024]{1,0:T(8,128)(2,1)}, bf16[768,1024]{1,0:T(8,128)(2,1)}, u32[]{:S(2)}, u32[]{:S(2)}) collective-permute-start(bf16[768,1024]{1,0:T(8,128)(2,1)} %constant_dynamic-update-slice_fusion), channel_id=1, source_target_pairs={{0,2},{1,3},{2,0},{3,1},{4,6},{5,7},{6,4},{7,5},{8,10},{9,11},{10,... | collective-permute-start | bytes 4718600 | tf_op jit(solution)/shard_map/ppermute | solution.py:526
  6.9 142.2 %collective-permute-start = (bf16[768,1024]{1,0:T(8,128)(2,1)}, bf16[768,1024]{1,0:T(8,128)(2,1)}, u32[]{:S(2)}, u32[]{:S(2)}) collective-permute-start(bf16[768,1024]{1,0:T(8,128)(2,1)} %constant_dynamic-update-slice_fusion), channel_id=1, source_target_pairs={{0,1},{1,0},{2,3},{3,2},{4,5},{5,4},{6,7},{7,6},{8,9},{9,8},{10,11... | collective-permute-start | bytes 4718600 | tf_op jit(solution)/shard_map/ppermute | solution.py:525
  7.3 2.0 copy-start.32
  7.4 2.8 copy-start.12
  74.9 1.5 copy-start.4
  76.4 1.6 copy-start.10
  78.0 39.0 %copy-start.6 = (bf16[192,768]{1,0:T(8,128)(2,1)S(1)}, bf16[192,768]{1,0:T(8,128)(2,1)}, u32[]{:S(2)}) copy-start(bf16[192,768]{1,0:T(8,128)(2,1)} %w_ref.3) | copy-start | bytes 884740
  117.0 1.2 copy-start.2
  118.2 22.6 %copy-start.13 = (bf16[512,768]{1,0:T(8,128)(2,1)S(1)}, bf16[512,768]{1,0:T(8,128)(2,1)}, u32[]{:S(2)}) copy-start(bf16[512,768]{1,0:T(8,128)(2,1)} %param.20) | copy-start | bytes 2359300
  141.3 10.2 %collective-permute-start.4 = (bf16[768,1024]{1,0:T(8,128)(2,1)}, bf16[768,1024]{1,0:T(8,128)(2,1)}, u32[]{:S(2)}, u32[]{:S(2)}) collective-permute-start(bf16[768,1024]{1,0:T(8,128)(2,1)} %collective-permute-done.2), channel_id=1, source_target_pairs={{0,1},{1,0},{2,3},{3,2},{4,5},{5,4},{6,7},{7,6},{8,9},{9,8},{10,11... | collective-permute-start | bytes 4718600 | tf_op jit(solution)/shard_map/ppermute | solution.py:525
  143.6 35.2 %copy-start.17 = (bf16[512,768]{1,0:T(8,128)(2,1)}, bf16[512,768]{1,0:T(8,128)(2,1)S(1)}, u32[]{:S(2)}) copy-start(bf16[512,768]{1,0:T(8,128)(2,1)S(1)} %multiply_convert_fusion) | copy-start | bytes 2359300
  146.3 13.6 %collective-permute-start.5 = (bf16[512,768]{1,0:T(8,128)(2,1)}, bf16[512,768]{1,0:T(8,128)(2,1)S(1)}, u32[]{:S(2)}, u32[]{:S(2)}) collective-permute-start(bf16[512,768]{1,0:T(8,128)(2,1)} %collective-permute-done.3), channel_id=1, source_target_pairs={{0,1},{1,0},{2,3},{3,2},{4,5},{5,4},{6,7},{7,6},{8,9},{9,8},{10,11... | collective-permute-start | bytes 2359304 | tf_op jit(solution)/shard_map/ppermute | solution.py:525
  153.9 1.8 copy-start.20
  155.8 2.3 copy-start.21
  158.1 1.8 copy-start.19
  160.7 7.7 %copy-start.15 = (bf16[512,768]{1,0:T(8,128)(2,1)}, bf16[512,768]{1,0:T(8,128)(2,1)S(1)}, u32[]{:S(2)}) copy-start(bf16[512,768]{1,0:T(8,128)(2,1)S(1)} %get-tuple-element.183) | copy-start | bytes 2359300
  164.4 162.9 %collective-permute-start.9 = (bf16[512,768]{1,0:T(8,128)(2,1)}, bf16[512,768]{1,0:T(8,128)(2,1)}, u32[]{:S(2)}, u32[]{:S(2)}) collective-permute-start(bf16[512,768]{1,0:T(8,128)(2,1)} %convolution_convert_fusion.4), channel_id=1, source_target_pairs={{0,1},{1,0},{2,3},{3,2},{4,5},{5,4},{6,7},{7,6},{8,9},{9,8},{10,11... | collective-permute-start | bytes 2359304 | tf_op jit(solution)/shard_map/ppermute | solution.py:525
  164.6 157.2 %collective-permute-start.10 = (bf16[512,768]{1,0:T(8,128)(2,1)}, bf16[512,768]{1,0:T(8,128)(2,1)}, u32[]{:S(2)}, u32[]{:S(2)}) collective-permute-start(bf16[512,768]{1,0:T(8,128)(2,1)} %convolution_convert_fusion.3), channel_id=1, source_target_pairs={{0,1},{1,0},{2,3},{3,2},{4,5},{5,4},{6,7},{7,6},{8,9},{9,8},{10,11... | collective-permute-start | bytes 2359304 | tf_op jit(solution)/shard_map/ppermute | solution.py:525
  173.4 3.2 copy-start.24
  173.4 3.2 copy-start.26
  173.4 10.0 %copy-start.35 = (bf16[512,512]{1,0:T(8,128)(2,1)}, bf16[512,512]{1,0:T(8,128)(2,1)S(1)}, u32[]{:S(2)}) copy-start(bf16[512,512]{1,0:T(8,128)(2,1)S(1)} %get-tuple-element.173) | copy-start | bytes 1572868
  173.4 10.0 %copy-start.36 = (bf16[512,512]{1,0:T(8,128)(2,1)}, bf16[512,512]{1,0:T(8,128)(2,1)S(1)}, u32[]{:S(2)}) copy-start(bf16[512,512]{1,0:T(8,128)(2,1)S(1)} %get-tuple-element.174) | copy-start | bytes 1572868
  188.8 186.6 %collective-permute-start.6 = (bf16[768,1024]{1,0:T(8,128)(2,1)}, bf16[768,1024]{1,0:T(8,128)(2,1)}, u32[]{:S(2)}, u32[]{:S(2)}) collective-permute-start(bf16[768,1024]{1,0:T(8,128)(2,1)} %convolution_convert_fusion.1), channel_id=1, source_target_pairs={{0,1},{1,0},{2,3},{3,2},{4,5},{5,4},{6,7},{7,6},{8,9},{9,8},{10,11... | collective-permute-start | bytes 4718600 | tf_op jit(solution)/shard_map/ppermute | solution.py:525
  188.9 128.2 %collective-permute-start.7 = (bf16[768,1024]{1,0:T(8,128)(2,1)}, bf16[768,1024]{1,0:T(8,128)(2,1)}, u32[]{:S(2)}, u32[]{:S(2)}) collective-permute-start(bf16[768,1024]{1,0:T(8,128)(2,1)} %convolution_convert_fusion), channel_id=1, source_target_pairs={{0,1},{1,0},{2,3},{3,2},{4,5},{5,4},{6,7},{7,6},{8,9},{9,8},{10,11... | collective-permute-start | bytes 4718600 | tf_op jit(solution)/shard_map/ppermute | solution.py:525
  213.9 1.0 copy-start.5
  214.9 1.7 copy-start.8
  282.7 1.7 copy-start.7
  284.5 22.5 %copy-start.14 = (bf16[512,768]{1,0:T(8,128)(2,1)S(1)}, bf16[512,768]{1,0:T(8,128)(2,1)}, u32[]{:S(2)}) copy-start(bf16[512,768]{1,0:T(8,128)(2,1)} %param.20) | copy-start | bytes 2359300
  284.5 23.2 %copy-start.11 = (bf16[2048,768]{1,0:T(8,128)(2,1)S(1)}, bf16[2048,768]{1,0:T(8,128)(2,1)}, u32[]{:S(2)}) copy-start(bf16[2048,768]{1,0:T(8,128)(2,1)} %copy-done.10) | copy-start | bytes 9437188
  307.7 3.1 copy-start.34
  310.8 5.8 %copy-start.16 = (bf16[512,768]{1,0:T(8,128)(2,1)S(1)}, bf16[512,768]{1,0:T(8,128)(2,1)}, u32[]{:S(2)}) copy-start(bf16[512,768]{1,0:T(8,128)(2,1)} %copy-done.15) | copy-start | bytes 2359300
  316.5 1.1 copy-start.18
  317.1 4.7 copy-start.22
  320.4 3.9 copy-start.25
  320.4 3.9 copy-start.27
  320.4 55.0 %collective-permute-start.8 = (bf16[768,1024]{1,0:T(8,128)(2,1)S(1)}, bf16[768,1024]{1,0:T(8,128)(2,1)S(1)}, u32[]{:S(2)}, u32[]{:S(2)}) collective-permute-start(bf16[768,1024]{1,0:T(8,128)(2,1)S(1)} %add_convert_fusion.1), channel_id=1, source_target_pairs={{0,2},{1,3},{2,0},{3,1},{4,6},{5,7},{6,4},{7,5},{8,10},{9,11},{10,... | collective-permute-start | bytes 4718600 | tf_op jit(solution)/shard_map/ppermute | solution.py:526
  323.5 49.4 %collective-permute-start.11 = (bf16[512,768]{1,0:T(8,128)(2,1)S(1)}, bf16[512,768]{1,0:T(8,128)(2,1)S(1)}, u32[]{:S(2)}, u32[]{:S(2)}) collective-permute-start(bf16[512,768]{1,0:T(8,128)(2,1)S(1)} %add_convert_fusion.3), channel_id=1, source_target_pairs={{0,2},{1,3},{2,0},{3,1},{4,6},{5,7},{6,4},{7,5},{8,10},{9,11},{10,... | collective-permute-start | bytes 2359304 | tf_op jit(solution)/shard_map/ppermute | solution.py:526
  324.3 1.2 copy-start.3
  324.3 2.2 copy-start.9
  499.9 2.1 copy-start.1
  (1 other events, 0.7 us)
